TPU v7x, 32 devices: a whole 2x2x4 slice. The times are simulated.
32 devices in a mesh: rows: 8 (over z, y), cols: 4 (over x, core).
Axes of the slice: x: 2, y: 2, z: 4, core: 2. Of those that a mesh axis runs over, the one named last changes fastest.
Arguments:
- tokens: bfloat16 [96, 96, 768], P('rows', 'cols'), may hold values from -48 to 48
- ln_gain: float32 [768], replicated, may hold values from 0.5 to 1.5
- ln_bias: float32 [768], replicated, may hold values from -3 to 3
- qkv_weight: bfloat16 [768, 2304], replicated, may hold values from -3 to 3
- qkv_bias: float32 [2304], replicated, may hold values from -3 to 3
- rel_table: float32 [23, 23, 24], replicated, may hold values from -4 to 4
- proj_weight: bfloat16 [768, 768], replicated, may hold values from -0.21875 to 0.21875
- proj_bias: float32 [768], replicated, may hold values from -3 to 3
- branch_weight: bfloat16 [4, 768, 512], replicated, may hold values from -0.21875 to 0.21875
- branch_bias: float32 [4, 512], replicated, may hold values from -4 to 4
- join_block: bfloat16 [768, 512], replicated, may hold values from -0.109375 to 0.109375
- join_branch: bfloat16 [4, 512, 512], replicated, may hold values from -0.375 to 0.375
- bn_gain: float32 [512], replicated, may hold values from 0.25 to 1.75
- bn_bias: float32 [512], replicated, may hold values from -4 to 4
Outputs:
- joined: bfloat16 [96, 96, 512], P('rows', 'cols')
All inputs are finite; a program needn't handle non-finite values.
Results may differ from a plain program's by a relative error of at most 0.0049.
Values may be sent and summed in bfloat16 or wider, within the bound.
No kernel may reach another device: no remote copies, remote signals or barrier semaphores. Data moves between devices by JAX's collectives and lax.ppermute only.
A program may use at most 128 MiB of HBM per device.

v0:
```python
import functools

import jax
import jax.numpy as jnp
import numpy as np
from jax import lax
from jax.experimental import pallas as pl
from jax.experimental.pallas import tpu as pltpu
from jax.sharding import PartitionSpec as P


WIN = 12
HALF = WIN // 2
bin_scales = (1, 2, 3, 6)
norm_eps = 1e-05
highest = lax.Precision.HIGHEST
f32 = jnp.float32
bf16 = jnp.bfloat16
axes = ("rows", "cols")


def up(count, step):
    return -(-count // step) * step


def window_order(row_count, col_count):
    order = []
    for wr in range(row_count // WIN):
        for wc in range(col_count // WIN):
            for p in range(WIN):
                for q in range(WIN):
                    order.append((wr * WIN + p, wc * WIN + q))
    return order


def piece_sizes(row_count, col_count):
    inner_r, inner_c = row_count - HALF, col_count - HALF
    sizes = [inner_r * inner_c, HALF * inner_c, inner_r * HALF, HALF * HALF]
    starts, at = [], 0
    for size in sizes:
        starts.append(at)
        at += up(size, 16)
    return sizes, starts, at


def tile_sizes(row_count, col_count):
    sizes = [row_count * col_count] + piece_sizes(row_count, col_count)[0][1:]
    starts, at = [], 0
    for size in sizes:
        starts.append(at)
        at += up(size, 16)
    return sizes, starts, at


def roll_send(row_count, col_count):
    inner_c = col_count - HALF
    _, starts, total = piece_sizes(row_count, col_count)
    base = starts[1]
    table = np.zeros((total - base, row_count * col_count), np.float32)
    for i in range(row_count):
        for j in range(col_count):
            if i < HALF and j >= HALF:
                target = starts[1] + i * inner_c + (j - HALF)
            elif i < HALF:
                target = starts[3] + i * HALF + j
            elif j < HALF:
                target = starts[2] + (i - HALF) * HALF + j
            else:
                continue
            table[target - base, i * col_count + j] = 1.0
    return table


def roll_gather(row_count, col_count):
    inner_r, inner_c = row_count - HALF, col_count - HALF
    _, starts, total = tile_sizes(row_count, col_count)
    table = np.zeros((row_count * col_count, total), np.float32)
    for token, (i, j) in enumerate(window_order(row_count, col_count)):
        if i < inner_r and j < inner_c:
            source = starts[0] + (i + HALF) * col_count + (j + HALF)
        elif j < inner_c:
            source = starts[1] + (i - inner_r) * inner_c + j
        elif i < inner_r:
            source = starts[2] + i * HALF + (j - inner_c)
        else:
            source = starts[3] + (i - inner_r) * HALF + (j - inner_c)
        table[token, source] = 1.0
    return table


def unroll_scatter(row_count, col_count):
    inner_r, inner_c = row_count - HALF, col_count - HALF
    _, starts, total = piece_sizes(row_count, col_count)
    table = np.zeros((total, row_count * col_count), np.float32)
    for token, (i, j) in enumerate(window_order(row_count, col_count)):
        if i < inner_r and j < inner_c:
            target = starts[0] + i * inner_c + j
        elif j < inner_c:
            target = starts[1] + (i - inner_r) * inner_c + j
        elif i < inner_r:
            target = starts[2] + i * HALF + (j - inner_c)
        else:
            target = starts[3] + (i - inner_r) * HALF + (j - inner_c)
        table[target, token] = 1.0
    return table


def unroll_gather(row_count, col_count):
    inner_c = col_count - HALF
    _, starts, total = piece_sizes(row_count, col_count)
    table = np.zeros((row_count * col_count, total), np.float32)
    for i in range(row_count):
        for j in range(col_count):
            if i >= HALF and j >= HALF:
                source = starts[0] + (i - HALF) * inner_c + (j - HALF)
            elif j >= HALF:
                source = starts[1] + i * inner_c + (j - HALF)
            elif i >= HALF:
                source = starts[2] + (i - HALF) * HALF + j
            else:
                source = starts[3] + i * HALF + j
            table[i * col_count + j, source] = 1.0
    return table


def cell_list():
    cells = []
    for s in bin_scales:
        for a in range(s):
            for b in range(s):
                cells.append((s, a, b))
    return cells


CELLS = cell_list()
NCELL = len(CELLS)
FINE = bin_scales[-1]
NFINE = FINE * FINE
CELL_PAD = up(NCELL + 1, 8)
FINE_PAD = up(NFINE, 8)


def cell_table(height, breadth):
    table = np.zeros((64, 8), np.float32)
    for k, (s, a, b) in enumerate(CELLS):
        table[k, :5] = (s / height, s / breadth, s - 1.0, a, b)
    table[NCELL:, 3] = -9.0
    return table


def fine_table(height, breadth):
    table = np.zeros((FINE_PAD, 8), np.float32)
    table[:, :4] = -1.0
    for a in range(FINE):
        for b in range(FINE):
            table[a * FINE + b, :4] = (
                a * (height // FINE),
                (a + 1) * (height // FINE),
                b * (breadth // FINE),
                (b + 1) * (breadth // FINE),
            )
    return table


def group_table():
    table = np.zeros((64, FINE_PAD), np.float32)
    for k, (s, a, b) in enumerate(CELLS):
        step = FINE // s
        for aa in range(a * step, (a + 1) * step):
            for bb in range(b * step, (b + 1) * step):
                table[k, aa * FINE + bb] = 1.0
    return table


def spread_weights(total, s):
    place = np.clip((np.arange(total) + 0.5) * s / total - 0.5, 0.0, s - 1.0)
    return np.maximum(0.0, 1.0 - np.abs(place[:, None] - np.arange(s)[None, :]))


def gram_tables(height, breadth):
    rows = np.zeros((height, 64))
    cols = np.zeros((breadth, 64))
    for k, (s, a, b) in enumerate(CELLS):
        rows[:, k] = spread_weights(height, s)[:, a]
        cols[:, k] = spread_weights(breadth, s)[:, b]
    gram = (rows.T @ rows) * (cols.T @ cols)
    mass = rows.sum(0) * cols.sum(0)
    gram[NCELL] = mass
    return gram.astype(np.float32)


def send_kernel(geo, tokens_ref, table_ref, rr_ref, rc_ref, rd_ref, tok_ref, tab_ref, sem):
    sizes, starts, _ = piece_sizes(geo[0], geo[1])
    copies = [
        pltpu.make_async_copy(tokens_ref, tok_ref, sem.at[0]),
        pltpu.make_async_copy(table_ref, tab_ref, sem.at[1]),
    ]
    for copy in copies:
        copy.start()
    for copy in copies:
        copy.wait()
    pieces = contract(tab_ref[...], tok_ref[...], ((1,), (0,))).astype(bf16)
    for ref, start, size in zip((rr_ref, rc_ref, rd_ref), starts[1:], sizes[1:]):
        at = start - starts[1]
        ref[...] = pieces[at : at + size]


def bias_kernel(count, table_ref, *refs):
    sources, out_ref = refs[:count], refs[count]
    targets = refs[count + 1 : 2 * count + 1]
    rel_ref, g_ref, sem = refs[2 * count + 1 :]
    copies = [
        pltpu.make_async_copy(source, target, sem.at[k])
        for k, (source, target) in enumerate(zip(sources, targets))
    ]
    for copy in copies:
        copy.start()
    heads = table_ref.shape[2]
    span = 2 * WIN - 1
    for a in range(span):
        rel_ref[:, a, :span] = table_ref[a].T
    lane = lax.broadcasted_iota(jnp.int32, (heads, 16, 128), 2)
    tiles = [jnp.zeros((heads, 16, 128), f32) for _ in range(3)]
    for a in range(span):
        line = rel_ref[:, a : a + 1, :]
        shift = (WIN * a - (WIN - 1)) % 128
        if shift > 112:
            line = pltpu.roll(line, shift, 2)
            shift = 0
        line = jnp.broadcast_to(line, (heads, 16, 128))
        moved = pltpu.roll(line, shift, 2, stride=1, stride_axis=1)
        first, last = WIN * a, WIN * a + WIN
        for t in range(first // 128, (last - 1) // 128 + 1):
            inside = (lane >= first - 128 * t) & (lane < last - 128 * t)
            tiles[t] = jnp.where(inside, moved, tiles[t])
    for t in range(3):
        g_ref[:, :, 128 * t : 128 * t + 128] = tiles[t]
    for u in range(WIN):
        offset = WIN * (WIN - 1 - u)
        wide = g_ref[...]
        if offset:
            wide = pltpu.roll(wide, 384 - offset, 2)
        out_ref[:, WIN * u : WIN * u + WIN, :] = wide[:, :WIN, : WIN * WIN]
    for copy in copies:
        copy.wait()


def expanded_bias(rel_table, *brought):
    heads = rel_table.shape[2]
    tokens = WIN * WIN
    vmem = pl.BlockSpec(memory_space=pltpu.VMEM)
    return pl.pallas_call(
        functools.partial(bias_kernel, len(brought)),
        out_shape=[jax.ShapeDtypeStruct((heads, tokens, tokens), f32)]
        + [jax.ShapeDtypeStruct(x.shape, x.dtype) for x in brought],
        in_specs=[vmem] + [pl.BlockSpec(memory_space=pltpu.HBM)] * len(brought),
        out_specs=[vmem] * (1 + len(brought)),
        scratch_shapes=[
            pltpu.VMEM((heads, 24, 128), f32),
            pltpu.VMEM((heads, 16, 384), f32),
            pltpu.SemaphoreType.DMA((len(brought),)),
        ],
        compiler_params=pltpu.CompilerParams(vmem_limit_bytes=16 << 20),
        cost_estimate=pl.CostEstimate(
            flops=4 * heads * tokens * tokens,
            bytes_accessed=4 * heads * tokens * 256,
            transcendentals=0,
        ),
        name="expand_bias",
    )(rel_table, *[pltpu.with_memory_space_constraint(x, pltpu.HBM) for x in brought])


def contract(a, b, dims, **kw):
    return lax.dot_general(a, b, (dims, ((), ())), preferred_element_type=f32, **kw)


def attention_kernel(
    geo,
    own_ref,
    rr_ref,
    rc_ref,
    rd_ref,
    gather_ref,
    scatter_ref,
    lng_ref,
    lnb_ref,
    wqkv_ref,
    bqkv_ref,
    bias_ref,
    wproj_ref,
    bproj_ref,
    wjoin_ref,
    small_ref,
    keep_ref,
    send_ref,
    o_own_ref,
    o_row_ref,
    o_col_ref,
    o_diag_ref,
    xs_ref,
    q_ref,
    k_ref,
    vt_ref,
    ct_ref,
    blk_ref,
    pen_ref,
    buf_ref,
    sa_ref,
    sb_ref,
    pa_ref,
    pb_ref,
):
    row_count, col_count, height, breadth = geo
    nwr, nwc = row_count // WIN, col_count // WIN
    tokens, width = row_count * col_count, own_ref.shape[1]
    wt = WIN * WIN
    heads = bias_ref.shape[0]
    hd = width // heads
    per_tile = 128 // hd
    my_row, my_col = lax.axis_index("rows"), lax.axis_index("cols")
    bit = lax.rem(my_col, 2)
    sizes, starts, total = tile_sizes(row_count, col_count)
    xs_ref[starts[1] :, :] = jnp.zeros((total - starts[1], width), bf16)
    for ref, start, size in zip((own_ref, rr_ref, rc_ref, rd_ref), starts, sizes):
        xs_ref[start : start + size, :] = ref[...]
    sizes, starts, total = piece_sizes(row_count, col_count)
    rolled = contract(gather_ref[...], xs_ref[...], ((1,), (0,)))
    center = jnp.mean(rolled, -1, keepdims=True)
    delta = rolled - center
    spread = jnp.mean(delta * delta, -1, keepdims=True)
    normed = (delta * lax.rsqrt(spread + norm_eps) * lng_ref[...][None, :] + lnb_ref[...][None, :]).astype(bf16)
    blk_ref[...] = rolled.astype(bf16)
    for part in range(3):
        cols = slice(part * width, (part + 1) * width)
        mixed = contract(normed, wqkv_ref[:, cols], ((1,), (0,))) + bqkv_ref[cols][None, :]
        if part == 0:
            q_ref[...] = (mixed * hd ** (-0.5)).astype(bf16).reshape(q_ref.shape)
        elif part == 1:
            k_ref[...] = mixed.astype(bf16).reshape(k_ref.shape)
        else:
            for w in range(nwr * nwc):
                vt_ref[w] = mixed[w * wt : (w + 1) * wt].T.astype(bf16)

    sub = lax.broadcasted_iota(jnp.int32, (wt, wt), 0)
    lane = lax.broadcasted_iota(jnp.int32, (wt, wt), 1)
    row_diff = (sub < wt // 2) != (lane < wt // 2)
    col_diff = (sub % WIN < HALF) != (lane % WIN < HALF)
    for wr in range(nwr):
        for wc in range(nwc):
            row_last = my_row * nwr + wr == height // WIN - 1
            col_last = my_col * nwc + wc == breadth // WIN - 1
            bad = (row_diff & row_last) | (col_diff & col_last)
            pen_ref[wr * nwc + wc] = jnp.where(bad, -100.0, 0.0)

    head_lane = lax.broadcasted_iota(jnp.int32, (wt, 128), 1) // hd
    tiles = width // 128
    steps = nwr * nwc * tiles

    def make_scores(step, s_ref):
        step = jnp.minimum(step, steps - 1)
        w, at = step // tiles, pl.multiple_of(step % tiles * 128, 128)
        queries = q_ref[w, :, pl.ds(at, 128)]
        keys = k_ref[w, :, pl.ds(at, 128)]
        for hh in range(per_tile):
            keys_h = jnp.where(head_lane == hh, keys, jnp.zeros_like(keys))
            s_ref[hh] = contract(keys_h, queries, ((1,), (1,)))

    def make_weights(step, s_ref, p_ref):
        w, t = step // tiles, step % tiles
        for hh in range(per_tile):
            scores = s_ref[hh] + bias_ref[t * per_tile + hh] + pen_ref[w]
            top = jnp.max(scores, 0, keepdims=True)
            grown = jnp.exp(scores - top)
            scale = 1.0 / jnp.sum(grown, 0, keepdims=True)
            p_ref[hh] = (grown * scale).astype(bf16)

    def make_context(step, p_ref):
        step = jnp.maximum(step, 0)
        w, at = step // tiles, step % tiles * 128
        for hh in range(per_tile):
            place = pl.multiple_of(at + hh * hd, hd)
            context = contract(vt_ref[w, pl.ds(place, hd), :], p_ref[hh], ((1,), (0,)))
            ct_ref[w, pl.ds(place, hd), :] = context.astype(bf16)

    def step_pair(pair, carry):
        step = pair * 2
        make_scores(step + 1, sb_ref)
        make_weights(step, sa_ref, pa_ref)
        make_context(step - 1, pb_ref)
        make_scores(step + 2, sa_ref)
        make_weights(step + 1, sb_ref, pb_ref)
        make_context(step, pa_ref)
        return carry

    make_scores(0, sa_ref)
    lax.fori_loop(0, steps // 2, step_pair, 0)
    make_context(steps - 1, pb_ref)

    for w in range(nwr * nwc):
        attended = contract(ct_ref[w], wproj_ref[...], ((0,), (0,))) + bproj_ref[...][None, :]
        here = slice(w * wt, (w + 1) * wt)
        blk_ref[here, :] = (blk_ref[here, :].astype(f32) + attended).astype(bf16)

    block = blk_ref[...]
    pieces = contract(scatter_ref[...], block, ((1,), (0,))).astype(bf16)
    for ref, start, size in zip((o_own_ref, o_row_ref, o_col_ref, o_diag_ref), starts, sizes):
        ref[...] = pieces[start : start + size]

    row = small_ref[0:1, :tokens] + (my_row * row_count + HALF).astype(f32)
    col = small_ref[1:2, :tokens] + (my_col * col_count + HALF).astype(f32)
    row = jnp.where(row >= height, row - height, row)
    col = jnp.where(col >= breadth, col - breadth, col)
    fine = small_ref[72 : 72 + FINE_PAD, :8]
    inside = (
        (row >= fine[:, 0:1]) & (row < fine[:, 1:2]) & (col >= fine[:, 2:3]) & (col < fine[:, 3:4])
    )
    pooled = contract(inside.astype(bf16), block, ((1,), (0,)))
    cell = small_ref[8 : 8 + CELL_PAD, :8]
    row_at = jnp.clip((row + 0.5) * cell[:, 0:1] - 0.5, 0.0, cell[:, 2:3])
    col_at = jnp.clip((col + 0.5) * cell[:, 1:2] - 0.5, 0.0, cell[:, 2:3])
    share = jnp.maximum(0.0, 1.0 - jnp.abs(row_at - cell[:, 3:4])) * jnp.maximum(
        0.0, 1.0 - jnp.abs(col_at - cell[:, 4:5])
    )
    direct = contract(block, wjoin_ref[...], ((1,), (0,)))
    weighted = contract(share, direct, ((1,), (0,)), precision=highest)
    squares = jnp.sum(direct * direct, 0, keepdims=True)
    which = lax.broadcasted_iota(jnp.int32, weighted.shape, 0)
    weighted = jnp.where(which == NCELL, squares, weighted)
    half_w, half_c = width // 2, direct.shape[1] // 2
    for b in range(2):
        at = 0
        for t in range(half_w // 128):
            lo = b * half_w + t * 128
            buf_ref[b, at : at + FINE_PAD, :] = pooled[:, lo : lo + 128]
            at += FINE_PAD
        for t in range(half_c // 128):
            lo = b * half_c + t * 128
            buf_ref[b, at : at + CELL_PAD, :] = weighted[:, lo : lo + 128]
            at += CELL_PAD
    keep_ref[...] = buf_ref[bit]
    send_ref[...] = buf_ref[1 - bit]


def half_rows(width, channels):
    return FINE_PAD * (width // 256) + CELL_PAD * (channels // 256)


def direct_kernel(
    geo, own_ref, rr_ref, rc_ref, rd_ref, gather_ref, wjoin_ref, token_ref, cell_ref,
    out_ref, share_ref, xs_ref
):
    row_count, col_count, _, _ = geo
    sizes, starts, _ = piece_sizes(row_count, col_count)
    my_row, my_col = lax.axis_index("rows"), lax.axis_index("cols")
    xs_ref[...] = jnp.zeros_like(xs_ref)
    for ref, start, size in zip((own_ref, rr_ref, rc_ref, rd_ref), starts, sizes):
        xs_ref[start : start + size, :] = ref[...]
    block = contract(gather_ref[...], xs_ref[...], ((1,), (0,))).astype(bf16)
    out_ref[...] = contract(block, wjoin_ref[...], ((1,), (0,)))
    row = token_ref[:, 0:1] + (my_row * row_count).astype(f32)
    col = token_ref[:, 1:2] + (my_col * col_count).astype(f32)
    row_at = jnp.clip((row + 0.5) * cell_ref[0:1, :] - 0.5, 0.0, cell_ref[2:3, :])
    col_at = jnp.clip((col + 0.5) * cell_ref[1:2, :] - 0.5, 0.0, cell_ref[2:3, :])
    share = jnp.maximum(0.0, 1.0 - jnp.abs(row_at - cell_ref[3:4, :])) * jnp.maximum(
        0.0, 1.0 - jnp.abs(col_at - cell_ref[4:5, :])
    )
    upper = share.astype(bf16)
    lower = (share - upper.astype(f32)).astype(bf16)
    lane = lax.broadcasted_iota(jnp.int32, share.shape, 1)
    share_ref[:, :128] = upper
    share_ref[:, 128:] = lower


def two_parts(value):
    upper = value.astype(bf16)
    return upper, (value - upper.astype(f32)).astype(bf16)


def final_kernel(
    geo,
    mine_ref,
    other_ref,
    direct_ref,
    share_ref,
    wb_ref,
    bb_ref,
    jb_ref,
    group_ref,
    gram_ref,
    gain_ref,
    bias_ref,
    out_ref,
    buf_ref,
    pool_ref,
    wei_ref,
    proj_ref,
):
    _, _, height, breadth = geo
    bit = lax.rem(lax.axis_index("cols"), 2)
    width, channels = pool_ref.shape[1], wei_ref.shape[1]
    half_w, half_c = width // 2, channels // 2
    buf_ref[bit] = mine_ref[...]
    buf_ref[1 - bit] = other_ref[...]
    for b in range(2):
        at = 0
        for t in range(half_w // 128):
            lo = b * half_w + t * 128
            pool_ref[:, lo : lo + 128] = buf_ref[b, at : at + FINE_PAD, :]
            at += FINE_PAD
        for t in range(half_c // 128):
            lo = b * half_c + t * 128
            wei_ref[:, lo : lo + 128] = buf_ref[b, at : at + CELL_PAD, :]
            at += CELL_PAD
    cells = contract(group_ref[...], pool_ref[...], ((1,), (0,)), precision=highest)
    proj_ref[...] = jnp.zeros_like(proj_ref)
    start = 0
    for k, s in enumerate(bin_scales):
        count = s * s
        scale = 1.0 / float((height // s) * (breadth // s))
        upper, lower = two_parts(cells[start : start + count] * scale)
        hidden = contract(upper, wb_ref[k], ((1,), (0,))) + contract(lower, wb_ref[k], ((1,), (0,)))
        hidden = jnp.maximum(hidden + bb_ref[k : k + 1, :], 0.0)
        upper, lower = two_parts(hidden)
        proj_ref[start : start + count, :] = contract(upper, jb_ref[k], ((1,), (0,))) + contract(
            lower, jb_ref[k], ((1,), (0,))
        )
        start += count
    projected = proj_ref[...]
    everyone = float(height * breadth)
    spun = contract(gram_ref[...], projected, ((1,), (0,)), precision=highest)
    weighted = wei_ref[...]
    lifted_sum = spun[NCELL : NCELL + 1]
    mixed = projected[:NCELL] * (spun[:NCELL] + 2.0 * weighted[:NCELL])
    mean_val = (weighted[0:1] + lifted_sum) * (1.0 / everyone)
    variance = (weighted[NCELL : NCELL + 1] + jnp.sum(mixed, 0, keepdims=True)) * (
        1.0 / everyone
    ) - mean_val * mean_val
    scale = lax.rsqrt(variance + norm_eps) * gain_ref[...][None, :]
    upper, lower = two_parts(projected)
    stack = jnp.concatenate([upper, lower], 0)
    lifted = contract(share_ref[:, :128], stack, ((1,), (0,))) + contract(
        share_ref[:, 128:], stack, ((1,), (0,))
    )
    joined = (direct_ref[...] + lifted - mean_val) * scale + bias_ref[...][None, :]
    out_ref[...] = jnp.maximum(joined, 0.0).astype(bf16)


def shards(
    tokens,
    ln_gain,
    ln_bias,
    qkv_weight,
    qkv_bias,
    rel_table,
    proj_weight,
    proj_bias,
    branch_weight,
    branch_bias,
    join_block,
    join_branch,
    bn_gain,
    bn_bias,
):
    row_count, col_count, width = tokens.shape
    nrow, ncol = lax.axis_size("rows"), lax.axis_size("cols")
    height, breadth = row_count * nrow, col_count * ncol
    geo = (row_count, col_count, height, breadth)
    channels = join_block.shape[1]
    count = row_count * col_count
    nwin = count // (WIN * WIN)
    everyone = nrow * ncol
    sizes, _, total = piece_sizes(row_count, col_count)

    def shifted(value, down, right):
        pairs = []
        for r in range(nrow):
            for c in range(ncol):
                pairs.append(
                    (r * ncol + c, ((r + down) % nrow) * ncol + (c + right) % ncol)
                )
        return lax.ppermute(value, axes, pairs)

    def exchanged(value, mask):
        return lax.ppermute(value, axes, [(i, i ^ mask) for i in range(everyone)])

    vmem = pl.BlockSpec(memory_space=pltpu.VMEM)
    hbm = pl.BlockSpec(memory_space=pltpu.HBM)

    shape = jax.ShapeDtypeStruct
    own = tokens.reshape(count, width)
    send_table = roll_send(row_count, col_count)
    send_rr, send_rc, send_rd = pl.pallas_call(
        functools.partial(send_kernel, geo),
        out_shape=[shape((size, width), bf16) for size in sizes[1:]],
        in_specs=[hbm] * 2,
        out_specs=[vmem] * 3,
        scratch_shapes=[
            pltpu.VMEM((count, width), bf16),
            pltpu.VMEM(send_table.shape, bf16),
            pltpu.SemaphoreType.DMA((2,)),
        ],
        compiler_params=pltpu.CompilerParams(vmem_limit_bytes=8 << 20),
        name="send_pieces",
    )(
        pltpu.with_memory_space_constraint(own, pltpu.HBM),
        pltpu.with_memory_space_constraint(jnp.asarray(send_table, bf16), pltpu.HBM),
    )
    rr = shifted(send_rr, -1, 0)
    rd = shifted(send_rd, -1, -1)
    rc = shifted(send_rc, 0, -1)

    order = np.array(window_order(row_count, col_count), np.float32)
    token_lanes = np.zeros((8, count), np.float32)
    token_lanes[:2] = order.T
    grid = np.zeros((count, 8), np.float32)
    grid[:, 0] = np.arange(count) // col_count
    grid[:, 1] = np.arange(count) % col_count
    cells = cell_table(height, breadth)
    cell_lanes = np.zeros((8, 128), np.float32)
    cell_lanes[:, :64] = cells.T
    cell_lanes[:, 64:] = cells.T
    rows_half = half_rows(width, channels)
    per_tile = 128 // (width // rel_table.shape[2])

    small = np.zeros((128, 384), np.float32)
    small[:8, :count] = token_lanes
    small[8:72, :8] = cells
    small[72 : 72 + FINE_PAD, :8] = fine_table(height, breadth)
    pair_bias, near_proj, near_join, near_gather, near_scatter, near_small, near_own = expanded_bias(
        rel_table,
        proj_weight,
        join_block,
        jnp.asarray(roll_gather(row_count, col_count), bf16),
        jnp.asarray(unroll_scatter(row_count, col_count), bf16),
        jnp.asarray(small),
        own,
    )
    keep, send, own_b, row_b, col_b, diag_b = pl.pallas_call(
        functools.partial(attention_kernel, geo),
        out_shape=[
            shape((rows_half, 128), f32),
            shape((rows_half, 128), f32),
        ]
        + [shape((size, width), bf16) for size in sizes],
        in_specs=[vmem] * 15,
        out_specs=[vmem] * 6,
        scratch_shapes=[
            pltpu.VMEM((tile_sizes(row_count, col_count)[2], width), bf16),
            pltpu.VMEM((nwin, WIN * WIN, width), bf16),
            pltpu.VMEM((nwin, WIN * WIN, width), bf16),
            pltpu.VMEM((nwin, width, WIN * WIN), bf16),
            pltpu.VMEM((nwin, width, WIN * WIN), bf16),
            pltpu.VMEM((count, width), bf16),
            pltpu.VMEM((nwin, WIN * WIN, WIN * WIN), f32),
            pltpu.VMEM((2, rows_half, 128), f32),
            pltpu.VMEM((per_tile, WIN * WIN, WIN * WIN), f32),
            pltpu.VMEM((per_tile, WIN * WIN, WIN * WIN), f32),
            pltpu.VMEM((per_tile, WIN * WIN, WIN * WIN), bf16),
            pltpu.VMEM((per_tile, WIN * WIN, WIN * WIN), bf16),
        ],
        compiler_params=pltpu.CompilerParams(vmem_limit_bytes=24 << 20),
        name="window_attention",
    )(
        near_own,
        rr,
        rc,
        rd,
        near_gather,
        near_scatter,
        ln_gain,
        ln_bias,
        qkv_weight,
        qkv_bias,
        pair_bias,
        near_proj,
        proj_bias,
        near_join,
        near_small,
    )

    rr_b = shifted(row_b, 1, 0)
    rd_b = shifted(diag_b, 1, 1)
    rc_b = shifted(col_b, 0, 1)
    mine = keep + exchanged(send, 1)
    mask = 2
    while mask < everyone:
        mine = mine + exchanged(mine, mask)
        mask *= 2
    other = exchanged(mine, 1)

    direct, share = pl.pallas_call(
        functools.partial(direct_kernel, geo),
        out_shape=[shape((count, channels), f32), shape((count, 256), bf16)],
        in_specs=[vmem] * 8,
        out_specs=[vmem] * 2,
        scratch_shapes=[pltpu.VMEM((total, width), bf16)],
        compiler_params=pltpu.CompilerParams(vmem_limit_bytes=16 << 20),
        cost_estimate=pl.CostEstimate(
            flops=2 * count * width * channels, bytes_accessed=4 << 20, transcendentals=0
        ),
        name="direct_join",
    )(
        own_b,
        rr_b,
        rc_b,
        rd_b,
        jnp.asarray(unroll_gather(row_count, col_count), bf16),
        join_block,
        jnp.asarray(grid),
        jnp.asarray(cell_lanes),
    )

    joined = pl.pallas_call(
        functools.partial(final_kernel, geo),
        out_shape=shape((count, channels), bf16),
        in_specs=[vmem] * 11,
        out_specs=vmem,
        scratch_shapes=[
            pltpu.VMEM((2, rows_half, 128), f32),
            pltpu.VMEM((FINE_PAD, width), f32),
            pltpu.VMEM((CELL_PAD, channels), f32),
            pltpu.VMEM((64, channels), f32),
        ],
        compiler_params=pltpu.CompilerParams(vmem_limit_bytes=24 << 20),
        name="final_join",
    )(
        mine,
        other,
        direct,
        share,
        branch_weight,
        branch_bias,
        join_branch,
        jnp.asarray(group_table()),
        jnp.asarray(gram_tables(height, breadth)),
        bn_gain,
        bn_bias,
    )
    return joined.reshape(row_count, col_count, channels)


def solution(mesh):
    in_specs = (P("rows", "cols", None),) + (P(),) * 13
    return jax.shard_map(
        shards, mesh=mesh, in_specs=in_specs, out_specs=P("rows", "cols", None), check_vma=False
    )
```

profile of v0, /device:TPU:0, one launch (start us, length us, event | category | flops | bytes accessed | tf_op | source)
XLA Modules:
  0.0 59.5 jit_solution(13288696841313821256)
XLA Ops:
  0.0 1.5 %send_pieces.1 = (bf16[108,768]{1,0:T(8,128)(2,1)S(1)}, bf16[36,768]{1,0:T(8,128)(2,1)S(1)}, bf16[36,768]{1,0:T(8,128)(2,1)S(1)}) custom-call(bf16[288,768]{1,0:T(8,128)(2,1)} %bitcast.2, bf16[208,288]{1,0:T(8,128)(2,1)} %constant.18.clone.table_ref), custom_call_target="tpu_custom_call" | custom-call | tf_op jit(solution)/shard_map/send_pieces/pallas_call | solution.py:592
  1.5 6.1 %collective-permute-start = (bf16[108,768]{1,0:T(8,128)(2,1)S(1)}, bf16[108,768]{1,0:T(8,128)(2,1)S(1)}, u32[]{:S(2)}, u32[]{:S(2)}) collective-permute-start(bf16[108,768]{1,0:T(8,128)(2,1)S(1)} %get-tuple-element.24), channel_id=1, source_target_pairs={{0,28},{1,29},{2,30},{3,31},{4,0},{5,1},{6,2},{7,3},{8,4},{9,5},{1... | collective-permute-start | bytes 497672 | tf_op jit(solution)/shard_map/ppermute | solution.py:581
  7.6 0.7 %collective-permute-start.1 = (bf16[36,768]{1,0:T(8,128)(2,1)S(1)}, bf16[36,768]{1,0:T(8,128)(2,1)S(1)}, u32[]{:S(2)}, u32[]{:S(2)}) collective-permute-start(bf16[36,768]{1,0:T(8,128)(2,1)S(1)} %get-tuple-element.25), channel_id=1, source_target_pairs={{0,3},{1,0},{2,1},{3,2},{4,7},{5,4},{6,5},{7,6},{8,11},{9,8},{10,9... | collective-permute-start | bytes 165896 | tf_op jit(solution)/shard_map/ppermute | solution.py:581
  8.3 0.9 %collective-permute-start.2 = (bf16[36,768]{1,0:T(8,128)(2,1)S(1)}, bf16[36,768]{1,0:T(8,128)(2,1)S(1)}, u32[]{:S(2)}, u32[]{:S(2)}) collective-permute-start(bf16[36,768]{1,0:T(8,128)(2,1)S(1)} %get-tuple-element.26), channel_id=1, source_target_pairs={{0,31},{1,28},{2,29},{3,30},{4,3},{5,0},{6,1},{7,2},{8,7},{9,4},{1... | collective-permute-start | bytes 165896 | tf_op jit(solution)/shard_map/ppermute | solution.py:581
  9.2 1.0 %copy-done.4 = f32[23,23,24]{2,1,0:T(8,128)S(1)} copy-done((f32[23,23,24]{2,1,0:T(8,128)S(1)}, f32[23,23,24]{2,1,0:T(8,128)}, u32[]{:S(2)}) %copy-start.4) | copy-done | bytes 50808
  10.2 4.1 %expand_bias.1 = (f32[24,144,144]{2,1,0:T(8,128)S(1)}, bf16[768,768]{1,0:T(8,128)(2,1)S(1)}, bf16[768,512]{1,0:T(8,128)(2,1)S(1)}, bf16[288,496]{1,0:T(8,128)(2,...) custom-call(f32[23,23,24]{2,1,0:T(8,128)S(1)} %copy-done.4, ...), custom_call_target="tpu_custom_call" | custom-call | flops 1990656 | bytes 3538944 | tf_op jit(solution)/shard_map/expand_bias/pallas_call | solution.py:252
  14.3 0.0 copy-start.2
  14.3 0.0 copy-start.5
  14.4 0.0 copy-start.6
  14.4 0.0 copy-start.14
  14.4 0.0 copy-start.3
  14.4 9.1 %window_attention.1 = (f32[232,128]{1,0:T(8,128)S(1)}, f32[232,128]{1,0:T(8,128)S(1)}, bf16[108,768]{1,0:T(8,128)(2,1)S(1)}, bf16[108,768]{1,0:T(8,128)(2,1)S(1)...) custom-call(bf16[288,768]{1,0:T(8,128)(2,1)S(1)} %get-tuple-element.23.own_ref, ...), custom_call_target="tpu_custom_call" | custom-call | tf_op jit(solution)/shard_map/window_attention/pallas_call | solution.py:638
  23.5 0.0 copy-start.1
  23.5 0.0 copy-start.7
  23.6 0.0 copy-start.8
  23.6 0.1 collective-permute-start.3
  23.7 1.3 %collective-permute-done.3 = f32[232,128]{1,0:T(8,128)S(1)} collective-permute-done((f32[232,128]{1,0:T(8,128)S(1)}, f32[232,128]{1,0:T(8,128)S(1)}, u32[]{:S(2)}, u32[]{:S(2)}) %collective-permute-start.3) | collective-permute-done | bytes 118816 | tf_op jit(solution)/shard_map/ppermute | solution.py:584
  25.0 0.6 %collective-permute-start.4 = (f32[232,128]{1,0:T(8,128)S(1)}, f32[232,128]{1,0:T(8,128)S(1)}, u32[]{:S(2)}, u32[]{:S(2)}) collective-permute-start(f32[232,128]{1,0:T(8,128)S(1)} %add.15), channel_id=1, source_target_pairs={{0,2},{1,3},{2,0},{3,1},{4,6},{5,7},{6,4},{7,5},{8,10},{9,11},{10,... | collective-permute-start | bytes 356360 | tf_op jit(solution)/shard_map/ppermute | solution.py:584
  25.6 4.8 %collective-permute-done.4 = f32[232,128]{1,0:T(8,128)S(1)} collective-permute-done((f32[232,128]{1,0:T(8,128)S(1)}, f32[232,128]{1,0:T(8,128)S(1)}, u32[]{:S(2)}, u32[]{:S(2)}) %collective-permute-start.4) | collective-permute-done | bytes 118816 | tf_op jit(solution)/shard_map/ppermute | solution.py:584
  30.4 1.6 %collective-permute-start.5 = (f32[232,128]{1,0:T(8,128)S(1)}, f32[232,128]{1,0:T(8,128)S(1)}, u32[]{:S(2)}, u32[]{:S(2)}) collective-permute-start(f32[232,128]{1,0:T(8,128)S(1)} %add.16), channel_id=1, source_target_pairs={{0,4},{1,5},{2,6},{3,7},{4,0},{5,1},{6,2},{7,3},{8,12},{9,13},{10,... | collective-permute-start | bytes 356360 | tf_op jit(solution)/shard_map/ppermute | solution.py:584
  32.0 3.3 %collective-permute-done.5 = f32[232,128]{1,0:T(8,128)S(1)} collective-permute-done((f32[232,128]{1,0:T(8,128)S(1)}, f32[232,128]{1,0:T(8,128)S(1)}, u32[]{:S(2)}, u32[]{:S(2)}) %collective-permute-start.5) | collective-permute-done | bytes 118816 | tf_op jit(solution)/shard_map/ppermute | solution.py:584
  35.3 0.1 collective-permute-start.6
  35.4 4.8 %collective-permute-done.6 = f32[232,128]{1,0:T(8,128)S(1)} collective-permute-done((f32[232,128]{1,0:T(8,128)S(1)}, f32[232,128]{1,0:T(8,128)S(1)}, u32[]{:S(2)}, u32[]{:S(2)}) %collective-permute-start.6) | collective-permute-done | bytes 118816 | tf_op jit(solution)/shard_map/ppermute | solution.py:584
  40.2 1.3 %collective-permute-start.7 = (f32[232,128]{1,0:T(8,128)S(1)}, f32[232,128]{1,0:T(8,128)S(1)}, u32[]{:S(2)}, u32[]{:S(2)}) collective-permute-start(f32[232,128]{1,0:T(8,128)S(1)} %add.18), channel_id=1, source_target_pairs={{0,16},{1,17},{2,18},{3,19},{4,20},{5,21},{6,22},{7,23},{8,24},{9,... | collective-permute-start | bytes 356360 | tf_op jit(solution)/shard_map/ppermute | solution.py:584
  41.5 1.9 %collective-permute-start.9 = (bf16[108,768]{1,0:T(8,128)(2,1)S(1)}, bf16[108,768]{1,0:T(8,128)(2,1)S(1)}, u32[]{:S(2)}, u32[]{:S(2)}) collective-permute-start(bf16[108,768]{1,0:T(8,128)(2,1)S(1)} %get-tuple-element.36), channel_id=1, source_target_pairs={{0,4},{1,5},{2,6},{3,7},{4,8},{5,9},{6,10},{7,11},{8,12},{9,13},{1... | collective-permute-start | bytes 497672 | tf_op jit(solution)/shard_map/ppermute | solution.py:581
  43.5 3.6 %collective-permute-done.7 = f32[232,128]{1,0:T(8,128)S(1)} collective-permute-done((f32[232,128]{1,0:T(8,128)S(1)}, f32[232,128]{1,0:T(8,128)S(1)}, u32[]{:S(2)}, u32[]{:S(2)}) %collective-permute-start.7) | collective-permute-done | bytes 118816 | tf_op jit(solution)/shard_map/ppermute | solution.py:584
  47.1 0.1 collective-permute-start.8
  47.2 0.5 collective-permute-start.10
  47.7 4.2 %collective-permute-start.11 = (bf16[36,768]{1,0:T(8,128)(2,1)S(1)}, bf16[36,768]{1,0:T(8,128)(2,1)S(1)}, u32[]{:S(2)}, u32[]{:S(2)}) collective-permute-start(bf16[36,768]{1,0:T(8,128)(2,1)S(1)} %get-tuple-element.38), channel_id=1, source_target_pairs={{0,5},{1,6},{2,7},{3,4},{4,9},{5,10},{6,11},{7,8},{8,13},{9,14},{1... | collective-permute-start | bytes 165896 | tf_op jit(solution)/shard_map/ppermute | solution.py:581
  51.8 3.6 %collective-permute-done.11.rd_ref = bf16[36,768]{1,0:T(8,128)(2,1)S(1)} collective-permute-done((bf16[36,768]{1,0:T(8,128)(2,1)S(1)}, bf16[36,768]{1,0:T(8,128)(2,1)S(1)}, u32[]{:S(2)}, u32[]{:S(2)}) %collective-permute-start.11) | collective-permute-done | bytes 55328 | tf_op jit(solution)/shard_map/ppermute | solution.py:581
  55.5 0.6 %direct_join.1 = (f32[288,512]{1,0:T(8,128)S(1)}, bf16[288,256]{1,0:T(8,128)(2,1)S(1)}) custom-call(bf16[108,768]{1,0:T(8,128)(2,1)S(1)} %get-tuple-element.35.own_ref, bf16[108,768]{1,0:T(8,128)(2,1)S(1)} %collective-permute-done.9.rr_ref, bf16[36,768]{1,0:T(8,128)(2,1)S(1)} %collective-permute-done.10.rc_ref, ...), custom_call_target="tpu_custom_call" | custom-call | flops 226492416 | bytes 4194304 | tf_op jit(solution)/shard_map/direct_join/pallas_call | solution.py:691
  56.2 3.3 %final_join.1 = bf16[288,512]{1,0:T(8,128)(2,1)} custom-call(f32[232,128]{1,0:T(8,128)S(1)} %add.19.mine_ref, f32[232,128]{1,0:T(8,128)S(1)} %collective-permute-done.8.other_ref, f32[288,512]{1,0:T(8,128)S(1)} %get-tuple-element.39.direct_ref, bf16[288,256]{1,0:T(8,128)(2,1)S(1)} %get-tuple-element.40.share_ref, bf16[4,768,512]{2,1,0:T(8,128)(2,1)S(1)} %copy-done.1, ...), custom_call_target="tpu_custom_call" | custom-call | tf_op jit(solution)/shard_map/final_join/pallas_call | solution.py:713
  (36 shorter events, 0.1 us)
Async XLA Ops:
  0.0 14.3 %copy-start = (bf16[768,2304]{1,0:T(8,128)(2,1)S(1)}, bf16[768,2304]{1,0:T(8,128)(2,1)}, u32[]{:S(2)}) copy-start(bf16[768,2304]{1,0:T(8,128)(2,1)} %wqkv_ref.1) | copy-start | bytes 10616836
  1.5 12.7 %collective-permute-start = (bf16[108,768]{1,0:T(8,128)(2,1)S(1)}, bf16[108,768]{1,0:T(8,128)(2,1)S(1)}, u32[]{:S(2)}, u32[]{:S(2)}) collective-permute-start(bf16[108,768]{1,0:T(8,128)(2,1)S(1)} %get-tuple-element.24), channel_id=1, source_target_pairs={{0,28},{1,29},{2,30},{3,31},{4,0},{5,1},{6,2},{7,3},{8,4},{9,5},{1... | collective-permute-start | bytes 497672 | tf_op jit(solution)/shard_map/ppermute | solution.py:581
  7.6 6.6 %collective-permute-start.1 = (bf16[36,768]{1,0:T(8,128)(2,1)S(1)}, bf16[36,768]{1,0:T(8,128)(2,1)S(1)}, u32[]{:S(2)}, u32[]{:S(2)}) collective-permute-start(bf16[36,768]{1,0:T(8,128)(2,1)S(1)} %get-tuple-element.25), channel_id=1, source_target_pairs={{0,3},{1,0},{2,1},{3,2},{4,7},{5,4},{6,5},{7,6},{8,11},{9,8},{10,9... | collective-permute-start | bytes 165896 | tf_op jit(solution)/shard_map/ppermute | solution.py:581
  8.3 6.0 %collective-permute-start.2 = (bf16[36,768]{1,0:T(8,128)(2,1)S(1)}, bf16[36,768]{1,0:T(8,128)(2,1)S(1)}, u32[]{:S(2)}, u32[]{:S(2)}) collective-permute-start(bf16[36,768]{1,0:T(8,128)(2,1)S(1)} %get-tuple-element.26), channel_id=1, source_target_pairs={{0,31},{1,28},{2,29},{3,30},{4,3},{5,0},{6,1},{7,2},{8,7},{9,4},{1... | collective-permute-start | bytes 165896 | tf_op jit(solution)/shard_map/ppermute | solution.py:581
  9.2 1.0 %copy-start.4 = (f32[23,23,24]{2,1,0:T(8,128)S(1)}, f32[23,23,24]{2,1,0:T(8,128)}, u32[]{:S(2)}) copy-start(f32[23,23,24]{2,1,0:T(8,128)} %table_ref.2) | copy-start | bytes 152356
  10.1 4.1 %copy-start.9 = (f32[2304]{0:T(1024)S(1)}, f32[2304]{0:T(1024)}, u32[]{:S(2)}) copy-start(f32[2304]{0:T(1024)} %bqkv_ref.1) | copy-start | bytes 27652
  10.1 4.2 %copy-start.11 = (f32[768]{0:T(1024)S(1)}, f32[768]{0:T(1024)}, u32[]{:S(2)}) copy-start(f32[768]{0:T(1024)} %lng_ref.1) | copy-start | bytes 9220
  10.1 4.2 %copy-start.12 = (f32[768]{0:T(1024)S(1)}, f32[768]{0:T(1024)}, u32[]{:S(2)}) copy-start(f32[768]{0:T(1024)} %lnb_ref.1) | copy-start | bytes 9220
  10.1 4.2 %copy-start.13 = (f32[768]{0:T(1024)S(1)}, f32[768]{0:T(1024)}, u32[]{:S(2)}) copy-start(f32[768]{0:T(1024)} %bproj_ref.1) | copy-start | bytes 9220
  14.3 41.1 %copy-start.2 = (bf16[768,512]{1,0:T(8,128)(2,1)S(1)}, bf16[768,512]{1,0:T(8,128)(2,1)}, u32[]{:S(2)}) copy-start(bf16[768,512]{1,0:T(8,128)(2,1)} %wjoin_ref.1) | copy-start | bytes 2359300
  14.3 41.1 %copy-start.5 = (bf16[288,320]{1,0:T(8,128)(2,1)S(1)}, bf16[288,320]{1,0:T(8,128)(2,1)}, u32[]{:S(2)}) copy-start(bf16[288,320]{1,0:T(8,128)(2,1)} %constant.22.clone.gather_ref) | copy-start | bytes 552964
  14.4 41.1 %copy-start.6 = (f32[288,8]{1,0:T(8,128)S(1)}, f32[288,8]{1,0:T(8,128)}, u32[]{:S(2)}) copy-start(f32[288,8]{1,0:T(8,128)} %constant.23.clone.token_ref) | copy-start | bytes 27652
  14.4 41.1 %copy-start.14 = (f32[8,128]{1,0:T(8,128)S(1)}, f32[8,128]{1,0:T(8,128)}, u32[]{:S(2)}) copy-start(f32[8,128]{1,0:T(8,128)} %constant.24.clone.cell_ref) | copy-start | bytes 12292
  14.4 41.7 %copy-start.3 = (bf16[4,512,512]{2,1,0:T(8,128)(2,1)S(1)}, bf16[4,512,512]{2,1,0:T(8,128)(2,1)}, u32[]{:S(2)}) copy-start(bf16[4,512,512]{2,1,0:T(8,128)(2,1)} %jb_ref.1) | copy-start | bytes 6291460
  23.5 32.6 %copy-start.1 = (bf16[4,768,512]{2,1,0:T(8,128)(2,1)S(1)}, bf16[4,768,512]{2,1,0:T(8,128)(2,1)}, u32[]{:S(2)}) copy-start(bf16[4,768,512]{2,1,0:T(8,128)(2,1)} %wb_ref.1) | copy-start | bytes 9437188
  23.5 32.6 %copy-start.7 = (f32[64,64]{1,0:T(8,128)S(1)}, f32[64,64]{1,0:T(8,128)}, u32[]{:S(2)}) copy-start(f32[64,64]{1,0:T(8,128)} %constant.26.clone.gram_ref) | copy-start | bytes 49156
  23.6 32.6 %copy-start.8 = (f32[64,40]{1,0:T(8,128)S(1)}, f32[64,40]{1,0:T(8,128)}, u32[]{:S(2)}) copy-start(f32[64,40]{1,0:T(8,128)} %constant.25.clone.group_ref) | copy-start | bytes 30724
  23.6 32.6 %copy-start.10 = (f32[4,512]{1,0:T(4,128)S(1)}, f32[4,512]{1,0:T(4,128)}, u32[]{:S(2)}) copy-start(f32[4,512]{1,0:T(4,128)} %bb_ref.1) | copy-start | bytes 24580
  23.6 32.6 %copy-start.15 = (f32[512]{0:T(512)S(1)}, f32[512]{0:T(512)}, u32[]{:S(2)}) copy-start(f32[512]{0:T(512)} %gain_ref.1) | copy-start | bytes 6148
  23.6 32.6 %copy-start.16 = (f32[512]{0:T(512)S(1)}, f32[512]{0:T(512)}, u32[]{:S(2)}) copy-start(f32[512]{0:T(512)} %bias_ref.1) | copy-start | bytes 6148
  23.6 1.4 %collective-permute-start.3 = (f32[232,128]{1,0:T(8,128)S(1)}, f32[232,128]{1,0:T(8,128)S(1)}, u32[]{:S(2)}, u32[]{:S(2)}) collective-permute-start(f32[232,128]{1,0:T(8,128)S(1)} %get-tuple-element.34), channel_id=1, source_target_pairs={{0,1},{1,0},{2,3},{3,2},{4,5},{5,4},{6,7},{7,6},{8,9},{9,8},{10,11... | collective-permute-start | bytes 356360 | tf_op jit(solution)/shard_map/ppermute | solution.py:584
  25.0 5.4 %collective-permute-start.4 = (f32[232,128]{1,0:T(8,128)S(1)}, f32[232,128]{1,0:T(8,128)S(1)}, u32[]{:S(2)}, u32[]{:S(2)}) collective-permute-start(f32[232,128]{1,0:T(8,128)S(1)} %add.15), channel_id=1, source_target_pairs={{0,2},{1,3},{2,0},{3,1},{4,6},{5,7},{6,4},{7,5},{8,10},{9,11},{10,... | collective-permute-start | bytes 356360 | tf_op jit(solution)/shard_map/ppermute | solution.py:584
  30.4 4.9 %collective-permute-start.5 = (f32[232,128]{1,0:T(8,128)S(1)}, f32[232,128]{1,0:T(8,128)S(1)}, u32[]{:S(2)}, u32[]{:S(2)}) collective-permute-start(f32[232,128]{1,0:T(8,128)S(1)} %add.16), channel_id=1, source_target_pairs={{0,4},{1,5},{2,6},{3,7},{4,0},{5,1},{6,2},{7,3},{8,12},{9,13},{10,... | collective-permute-start | bytes 356360 | tf_op jit(solution)/shard_map/ppermute | solution.py:584
  35.3 4.9 %collective-permute-start.6 = (f32[232,128]{1,0:T(8,128)S(1)}, f32[232,128]{1,0:T(8,128)S(1)}, u32[]{:S(2)}, u32[]{:S(2)}) collective-permute-start(f32[232,128]{1,0:T(8,128)S(1)} %add.17), channel_id=1, source_target_pairs={{0,8},{1,9},{2,10},{3,11},{4,12},{5,13},{6,14},{7,15},{8,0},{9,1},... | collective-permute-start | bytes 356360 | tf_op jit(solution)/shard_map/ppermute | solution.py:584
  40.2 6.9 %collective-permute-start.7 = (f32[232,128]{1,0:T(8,128)S(1)}, f32[232,128]{1,0:T(8,128)S(1)}, u32[]{:S(2)}, u32[]{:S(2)}) collective-permute-start(f32[232,128]{1,0:T(8,128)S(1)} %add.18), channel_id=1, source_target_pairs={{0,16},{1,17},{2,18},{3,19},{4,20},{5,21},{6,22},{7,23},{8,24},{9,... | collective-permute-start | bytes 356360 | tf_op jit(solution)/shard_map/ppermute | solution.py:584
  41.5 13.9 %collective-permute-start.9 = (bf16[108,768]{1,0:T(8,128)(2,1)S(1)}, bf16[108,768]{1,0:T(8,128)(2,1)S(1)}, u32[]{:S(2)}, u32[]{:S(2)}) collective-permute-start(bf16[108,768]{1,0:T(8,128)(2,1)S(1)} %get-tuple-element.36), channel_id=1, source_target_pairs={{0,4},{1,5},{2,6},{3,7},{4,8},{5,9},{6,10},{7,11},{8,12},{9,13},{1... | collective-permute-start | bytes 497672 | tf_op jit(solution)/shard_map/ppermute | solution.py:581
  47.1 9.0 %collective-permute-start.8 = (f32[232,128]{1,0:T(8,128)S(1)}, f32[232,128]{1,0:T(8,128)S(1)}, u32[]{:S(2)}, u32[]{:S(2)}) collective-permute-start(f32[232,128]{1,0:T(8,128)S(1)} %add.19.mine_ref), channel_id=1, source_target_pairs={{0,1},{1,0},{2,3},{3,2},{4,5},{5,4},{6,7},{7,6},{8,9},{9,8},{10,11... | collective-permute-start | bytes 356360 | tf_op jit(solution)/shard_map/ppermute | solution.py:584
  47.2 4.7 %collective-permute-start.10 = (bf16[36,768]{1,0:T(8,128)(2,1)S(1)}, bf16[36,768]{1,0:T(8,128)(2,1)S(1)}, u32[]{:S(2)}, u32[]{:S(2)}) collective-permute-start(bf16[36,768]{1,0:T(8,128)(2,1)S(1)} %get-tuple-element.37), channel_id=1, source_target_pairs={{0,1},{1,2},{2,3},{3,0},{4,5},{5,6},{6,7},{7,4},{8,9},{9,10},{10,1... | collective-permute-start | bytes 165896 | tf_op jit(solution)/shard_map/ppermute | solution.py:581
  47.7 7.7 %collective-permute-start.11 = (bf16[36,768]{1,0:T(8,128)(2,1)S(1)}, bf16[36,768]{1,0:T(8,128)(2,1)S(1)}, u32[]{:S(2)}, u32[]{:S(2)}) collective-permute-start(bf16[36,768]{1,0:T(8,128)(2,1)S(1)} %get-tuple-element.38), channel_id=1, source_target_pairs={{0,5},{1,6},{2,7},{3,4},{4,9},{5,10},{6,11},{7,8},{8,13},{9,14},{1... | collective-permute-start | bytes 165896 | tf_op jit(solution)/shard_map/ppermute | solution.py:581
where the time goes:
time: 59.6 us; the launch traced here: 59.5 us
  waiting for transfers between devices  21.4 us (36%)
  Pallas kernels  18.7 us (31%)
  starting transfers between devices  17.9 us (30%)
  local copies, waits for them, and re-layouts  1.05 us (2%)
    ppermute x6, waiting for transfers between devices, exchanged(): return lax.ppermute(value, axes, [(i, i ^ mask) for i in range(everyone)])  17.8 us
    ppermute x6, starting transfers between devices, shifted(): return lax.ppermute(value, axes, pairs)  14.2 us
    pallas_call x1, Pallas kernels, shards(): pl.pallas_call(functools.partial(attention_kernel, geo), out_shape=[shape...  9.14 us
    pallas_call x1, Pallas kernels, expanded_bias(): pl.pallas_call(functools.partial(bias_kernel, len(brought)), out_shape=[j...  4.09 us
    ppermute x6, starting transfers between devices, exchanged(): return lax.ppermute(value, axes, [(i, i ^ mask) for i in range(everyone)])  3.72 us
    ppermute x6, waiting for transfers between devices, shifted(): return lax.ppermute(value, axes, pairs)  3.6 us
    pallas_call x1, Pallas kernels, shards(): pl.pallas_call(functools.partial(final_kernel, geo), out_shape=shape((cou...  3.29 us
    pallas_call x1, Pallas kernels, shards(): pl.pallas_call(functools.partial(send_kernel, geo), out_shape=[shape((siz...  1.54 us
  transfers between devices with their start and end apart: 12, of which 6 were waited for; matrix products, arithmetic and copies ran while one was open for 0% of the time, Pallas kernels for 8%

commit v1 on v0

--- a/solution.py
+++ b/solution.py
@@ -13,10 +13,11 @@
 HALF = WIN // 2
 bin_scales = (1, 2, 3, 6)
 norm_eps = 1e-05
-highest = lax.Precision.HIGHEST
 f32 = jnp.float32
 bf16 = jnp.bfloat16
 axes = ("rows", "cols")
+TAIL = WIN * WIN - 128
+GROUP = 128 // TAIL
 
 
 def up(count, step):
@@ -136,15 +137,33 @@
 NCELL = len(CELLS)
 FINE = bin_scales[-1]
 NFINE = FINE * FINE
-CELL_PAD = up(NCELL + 1, 8)
 FINE_PAD = up(NFINE, 8)
-
-
-def cell_table(height, breadth):
+SENT = [k for k, (s, _, _) in enumerate(CELLS) if s == FINE or (s > 1 and (FINE // s) % 2 == 0)]
+NSENT = len(SENT)
+CELL_PAD = up(NSENT + 1, 8)
+
+
+def cell_table(height, breadth, sent):
+    chosen = [CELLS[k] for k in SENT] if sent else CELLS
     table = np.zeros((64, 8), np.float32)
+    for k, (s, a, b) in enumerate(chosen):
+        table[k, :5] = (s / height, s / breadth, s - 1.0, a, b)
+    table[len(chosen) :, 3] = -9.0
+    return table
+
+
+def spread_table():
+    table = np.zeros((64, CELL_PAD), np.float32)
     for k, (s, a, b) in enumerate(CELLS):
-        table[k, :5] = (s / height, s / breadth, s - 1.0, a, b)
-    table[NCELL:, 3] = -9.0
+        if k in SENT:
+            table[k, SENT.index(k)] = 1.0
+            continue
+        for m, sent in enumerate(SENT):
+            t, aa, bb = CELLS[sent]
+            if t == FINE:
+                row = np.clip((aa + 0.5) * s / FINE - 0.5, 0.0, s - 1.0)
+                col = np.clip((bb + 0.5) * s / FINE - 0.5, 0.0, s - 1.0)
+                table[k, m] = max(0.0, 1.0 - abs(row - a)) * max(0.0, 1.0 - abs(col - b))
     return table
 
 
@@ -162,14 +181,25 @@
     return table
 
 
+def cell_slots():
+    slots, at = [], 0
+    for s in bin_scales:
+        slots.append((at, up(s * s, 8)))
+        at += up(s * s, 8)
+    return slots, at
+
+
 def group_table():
-    table = np.zeros((64, FINE_PAD), np.float32)
-    for k, (s, a, b) in enumerate(CELLS):
+    slots, total = cell_slots()
+    table = np.zeros((total, FINE_PAD), np.float32)
+    for (first, _), s in zip(slots, bin_scales):
         step = FINE // s
-        for aa in range(a * step, (a + 1) * step):
-            for bb in range(b * step, (b + 1) * step):
-                table[k, aa * FINE + bb] = 1.0
-    return table
+        for a in range(s):
+            for b in range(s):
+                for aa in range(a * step, (a + 1) * step):
+                    for bb in range(b * step, (b + 1) * step):
+                        table[first + a * s + b, aa * FINE + bb] = 1.0
+    return np.concatenate([table] * 3, 1)
 
 
 def spread_weights(total, s):
@@ -186,14 +216,26 @@
     gram = (rows.T @ rows) * (cols.T @ cols)
     mass = rows.sum(0) * cols.sum(0)
     gram[NCELL] = mass
-    return gram.astype(np.float32)
-
-
-def send_kernel(geo, tokens_ref, table_ref, rr_ref, rc_ref, rd_ref, tok_ref, tab_ref, sem):
+    both = np.zeros((up(64 + CELL_PAD, 16), 64))
+    both[:64] = gram
+    both[64 : 64 + NSENT] = spread_table().T[:NSENT]
+    parts = []
+    for _ in range(3):
+        part = both.astype(jnp.bfloat16).astype(np.float64)
+        parts.append(part)
+        both = both - part
+    table = np.concatenate(parts, 0)
+    return np.concatenate([table] * 3, 1).astype(np.float32)
+
+
+def send_kernel(
+    geo, tokens_ref, table_ref, rel_ref, rr_ref, rc_ref, rd_ref, rel_out_ref, tok_ref, tab_ref, sem
+):
     sizes, starts, _ = piece_sizes(geo[0], geo[1])
     copies = [
         pltpu.make_async_copy(tokens_ref, tok_ref, sem.at[0]),
         pltpu.make_async_copy(table_ref, tab_ref, sem.at[1]),
+        pltpu.make_async_copy(rel_ref, rel_out_ref, sem.at[2]),
     ]
     for copy in copies:
         copy.start()
@@ -208,7 +250,7 @@
 def bias_kernel(count, table_ref, *refs):
     sources, out_ref = refs[:count], refs[count]
     targets = refs[count + 1 : 2 * count + 1]
-    rel_ref, g_ref, sem = refs[2 * count + 1 :]
+    line_ref, sem = refs[2 * count + 1 :]
     copies = [
         pltpu.make_async_copy(source, target, sem.at[k])
         for k, (source, target) in enumerate(zip(sources, targets))
@@ -217,30 +259,53 @@
         copy.start()
     heads = table_ref.shape[2]
     span = 2 * WIN - 1
+    line_ref[...] = jnp.zeros_like(line_ref)
     for a in range(span):
-        rel_ref[:, a, :span] = table_ref[a].T
-    lane = lax.broadcasted_iota(jnp.int32, (heads, 16, 128), 2)
-    tiles = [jnp.zeros((heads, 16, 128), f32) for _ in range(3)]
-    for a in range(span):
-        line = rel_ref[:, a : a + 1, :]
-        shift = (WIN * a - (WIN - 1)) % 128
-        if shift > 112:
-            line = pltpu.roll(line, shift, 2)
-            shift = 0
-        line = jnp.broadcast_to(line, (heads, 16, 128))
-        moved = pltpu.roll(line, shift, 2, stride=1, stride_axis=1)
-        first, last = WIN * a, WIN * a + WIN
-        for t in range(first // 128, (last - 1) // 128 + 1):
-            inside = (lane >= first - 128 * t) & (lane < last - 128 * t)
-            tiles[t] = jnp.where(inside, moved, tiles[t])
-    for t in range(3):
-        g_ref[:, :, 128 * t : 128 * t + 128] = tiles[t]
-    for u in range(WIN):
-        offset = WIN * (WIN - 1 - u)
-        wide = g_ref[...]
-        if offset:
-            wide = pltpu.roll(wide, 384 - offset, 2)
-        out_ref[:, WIN * u : WIN * u + WIN, :] = wide[:, :WIN, : WIN * WIN]
+        line_ref[a % 2, :, WIN * a : WIN * a + span] = table_ref[a].T
+    wide = [
+        [
+            jnp.broadcast_to(line_ref[par, :, 128 * t : 128 * t + 128][:, None, :], (heads, 8, 128))
+            for t in range(3)
+        ]
+        for par in range(2)
+    ]
+    lane = lax.broadcasted_iota(jnp.int32, (8, 128), 1)
+    sub = lax.broadcasted_iota(jnp.int32, (8, 128), 0)
+    tail = WIN * WIN - 128
+    per_slot = 128 // tail
+    for k in range(WIN * WIN // 8):
+        base = WIN * WIN - 8 - 8 * k
+        tile, rest = base // 128, base % 128
+        moved = []
+        for par in range(2):
+            rolled = [
+                pltpu.roll(wide[par][t], 121 - rest, 2, stride=1, stride_axis=1)
+                for t in range(tile, min(tile + 3, 3))
+            ]
+            near = lane < 121 - rest + sub
+            first = jnp.where(near[None], rolled[0], rolled[1])
+            second = rolled[1]
+            if rest + 7 + tail > 128:
+                second = jnp.where(near[None], rolled[1], rolled[2])
+            moved.append((first, second))
+        u = (8 * k + sub) // WIN
+        rows = slice(8 * k, 8 * k + 8)
+        for half in range(2):
+            odd = ((128 * half + lane) // WIN + u) % 2 == 1
+            result = jnp.where(odd[None], moved[0][half], moved[1][half])
+            for g in range(heads // per_slot):
+                part = result[g * per_slot : (g + 1) * per_slot]
+                slot = g * (per_slot + 1)
+                if half == 0:
+                    out_ref[slot : slot + per_slot, rows, :] = part
+                    continue
+                part = jnp.where((lane < tail)[None], part, 0.0)
+                pieces = [part[0]] + [
+                    pltpu.roll(part[h], tail * h, 1) for h in range(1, per_slot)
+                ]
+                while len(pieces) > 1:
+                    pieces = [x + y for x, y in zip(pieces[::2], pieces[1::2])]
+                out_ref[slot + per_slot, rows, :] = pieces[0]
     for copy in copies:
         copy.wait()
 
@@ -251,19 +316,18 @@
     vmem = pl.BlockSpec(memory_space=pltpu.VMEM)
     return pl.pallas_call(
         functools.partial(bias_kernel, len(brought)),
-        out_shape=[jax.ShapeDtypeStruct((heads, tokens, tokens), f32)]
+        out_shape=[jax.ShapeDtypeStruct((heads // GROUP * (GROUP + 1), tokens, 128), f32)]
         + [jax.ShapeDtypeStruct(x.shape, x.dtype) for x in brought],
         in_specs=[vmem] + [pl.BlockSpec(memory_space=pltpu.HBM)] * len(brought),
         out_specs=[vmem] * (1 + len(brought)),
         scratch_shapes=[
-            pltpu.VMEM((heads, 24, 128), f32),
-            pltpu.VMEM((heads, 16, 384), f32),
+            pltpu.VMEM((2, heads, 384), f32),
             pltpu.SemaphoreType.DMA((len(brought),)),
         ],
         compiler_params=pltpu.CompilerParams(vmem_limit_bytes=16 << 20),
         cost_estimate=pl.CostEstimate(
             flops=4 * heads * tokens * tokens,
-            bytes_accessed=4 * heads * tokens * 256,
+            bytes_accessed=4 * heads * tokens * 144,
             transcendentals=0,
         ),
         name="expand_bias",
@@ -272,6 +336,18 @@
 
 def contract(a, b, dims, **kw):
     return lax.dot_general(a, b, (dims, ((), ())), preferred_element_type=f32, **kw)
+
+
+def f32_parts(value):
+    first = value.astype(bf16).astype(f32)
+    rest = value - first
+    second = rest.astype(bf16).astype(f32)
+    return [first, second, (rest - second).astype(bf16).astype(f32)]
+
+
+def folded(value):
+    count = value.shape[0] // 3
+    return value[:count] + (value[count : 2 * count] + value[2 * count :])
 
 
 def attention_kernel(
@@ -314,7 +390,7 @@
     nwr, nwc = row_count // WIN, col_count // WIN
     tokens, width = row_count * col_count, own_ref.shape[1]
     wt = WIN * WIN
-    heads = bias_ref.shape[0]
+    heads = bias_ref.shape[0] // (GROUP + 1) * GROUP
     hd = width // heads
     per_tile = 128 // hd
     my_row, my_col = lax.axis_index("rows"), lax.axis_index("cols")
@@ -341,46 +417,63 @@
             for w in range(nwr * nwc):
                 vt_ref[w] = mixed[w * wt : (w + 1) * wt].T.astype(bf16)
 
-    sub = lax.broadcasted_iota(jnp.int32, (wt, wt), 0)
-    lane = lax.broadcasted_iota(jnp.int32, (wt, wt), 1)
-    row_diff = (sub < wt // 2) != (lane < wt // 2)
-    col_diff = (sub % WIN < HALF) != (lane % WIN < HALF)
-    for wr in range(nwr):
-        for wc in range(nwc):
-            row_last = my_row * nwr + wr == height // WIN - 1
-            col_last = my_col * nwc + wc == breadth // WIN - 1
-            bad = (row_diff & row_last) | (col_diff & col_last)
-            pen_ref[wr * nwc + wc] = jnp.where(bad, -100.0, 0.0)
+    sub = lax.broadcasted_iota(jnp.int32, (wt, 128), 0)
+    lane = lax.broadcasted_iota(jnp.int32, (wt, 128), 1)
+    for kind, query in enumerate((lane, 128 + lane % TAIL)):
+        row_diff = (sub < wt // 2) != (query < wt // 2)
+        col_diff = (sub % WIN < HALF) != (query % WIN < HALF)
+        for wr in range(nwr):
+            for wc in range(nwc):
+                row_last = my_row * nwr + wr == height // WIN - 1
+                col_last = my_col * nwc + wc == breadth // WIN - 1
+                bad = (row_diff & row_last) | (col_diff & col_last)
+                pen_ref[kind, wr * nwc + wc] = jnp.where(bad, -100.0, 0.0)
 
     head_lane = lax.broadcasted_iota(jnp.int32, (wt, 128), 1) // hd
-    tiles = width // 128
-    steps = nwr * nwc * tiles
+    span = GROUP * hd
+    joint_shape = (GROUP * TAIL, span)
+    joint_own = (
+        lax.broadcasted_iota(jnp.int32, joint_shape, 0) // TAIL
+        == lax.broadcasted_iota(jnp.int32, joint_shape, 1) // hd
+    )
+    groups = heads // GROUP
+    steps = nwr * nwc * groups
 
     def make_scores(step, s_ref):
         step = jnp.minimum(step, steps - 1)
-        w, at = step // tiles, pl.multiple_of(step % tiles * 128, 128)
-        queries = q_ref[w, :, pl.ds(at, 128)]
-        keys = k_ref[w, :, pl.ds(at, 128)]
-        for hh in range(per_tile):
-            keys_h = jnp.where(head_lane == hh, keys, jnp.zeros_like(keys))
-            s_ref[hh] = contract(keys_h, queries, ((1,), (1,)))
+        w, g = step // groups, step % groups
+        for h in range(GROUP):
+            at = pl.multiple_of(g * span + h // per_tile * 128, 128)
+            keys = k_ref[w, :, pl.ds(at, 128)]
+            keys = jnp.where(head_lane == h % per_tile, keys, jnp.zeros_like(keys))
+            s_ref[h] = contract(keys, q_ref[w, :128, pl.ds(at, 128)], ((1,), (1,)))
+        at = pl.multiple_of(g * span, span)
+        joint = jnp.concatenate([q_ref[w, 128:, pl.ds(at, span)]] * GROUP, 0)
+        joint = jnp.where(joint_own, joint, jnp.zeros_like(joint))
+        s_ref[GROUP] = contract(k_ref[w, :, pl.ds(at, span)], joint, ((1,), (1,)))
 
     def make_weights(step, s_ref, p_ref):
-        w, t = step // tiles, step % tiles
-        for hh in range(per_tile):
-            scores = s_ref[hh] + bias_ref[t * per_tile + hh] + pen_ref[w]
+        w, g = step // groups, step % groups
+        for h in range(GROUP + 1):
+            scores = s_ref[h] + bias_ref[g * (GROUP + 1) + h] + pen_ref[h // GROUP, w]
             top = jnp.max(scores, 0, keepdims=True)
             grown = jnp.exp(scores - top)
             scale = 1.0 / jnp.sum(grown, 0, keepdims=True)
-            p_ref[hh] = (grown * scale).astype(bf16)
+            p_ref[h] = (grown * scale).astype(bf16)
 
     def make_context(step, p_ref):
         step = jnp.maximum(step, 0)
-        w, at = step // tiles, step % tiles * 128
-        for hh in range(per_tile):
-            place = pl.multiple_of(at + hh * hd, hd)
-            context = contract(vt_ref[w, pl.ds(place, hd), :], p_ref[hh], ((1,), (0,)))
-            ct_ref[w, pl.ds(place, hd), :] = context.astype(bf16)
+        w, g = step // groups, step % groups
+        first = pl.multiple_of(g * span, span)
+        joint = contract(vt_ref[w, pl.ds(first, span), :], p_ref[GROUP], ((1,), (0,)))
+        for h in range(GROUP):
+            place = pl.multiple_of(first + h * hd, hd)
+            context = contract(vt_ref[w, pl.ds(place, hd), :], p_ref[h], ((1,), (0,)))
+            ct_ref[w, pl.ds(place, hd), :128] = context.astype(bf16)
+            rest = joint[h * hd : (h + 1) * hd]
+            if h:
+                rest = pltpu.roll(rest, 128 - TAIL * h, 1)
+            ct_ref[w, pl.ds(place, hd), 128:] = rest[:, :TAIL].astype(bf16)
 
     def step_pair(pair, carry):
         step = pair * 2
@@ -414,35 +507,41 @@
     inside = (
         (row >= fine[:, 0:1]) & (row < fine[:, 1:2]) & (col >= fine[:, 2:3]) & (col < fine[:, 3:4])
     )
-    pooled = contract(inside.astype(bf16), block, ((1,), (0,)))
     cell = small_ref[8 : 8 + CELL_PAD, :8]
     row_at = jnp.clip((row + 0.5) * cell[:, 0:1] - 0.5, 0.0, cell[:, 2:3])
     col_at = jnp.clip((col + 0.5) * cell[:, 1:2] - 0.5, 0.0, cell[:, 2:3])
     share = jnp.maximum(0.0, 1.0 - jnp.abs(row_at - cell[:, 3:4])) * jnp.maximum(
         0.0, 1.0 - jnp.abs(col_at - cell[:, 4:5])
     )
-    direct = contract(block, wjoin_ref[...], ((1,), (0,)))
-    weighted = contract(share, direct, ((1,), (0,)), precision=highest)
+    picks = jnp.concatenate([inside.astype(f32), *f32_parts(share)], 0).astype(bf16)
+    picked = contract(picks, block, ((1,), (0,)))
+    pooled = picked[:FINE_PAD]
+    lifted = folded(picked[FINE_PAD:])
+    both = jnp.concatenate([block, jnp.concatenate(f32_parts(lifted), 0).astype(bf16)], 0)
+    joined = contract(both, wjoin_ref[...], ((1,), (0,)))
+    direct, weighted = joined[:tokens], folded(joined[tokens:])
     squares = jnp.sum(direct * direct, 0, keepdims=True)
     which = lax.broadcasted_iota(jnp.int32, weighted.shape, 0)
-    weighted = jnp.where(which == NCELL, squares, weighted)
+    weighted = jnp.where(which == NSENT, squares, weighted)
     half_w, half_c = width // 2, direct.shape[1] // 2
     for b in range(2):
         at = 0
         for t in range(half_w // 128):
             lo = b * half_w + t * 128
-            buf_ref[b, at : at + FINE_PAD, :] = pooled[:, lo : lo + 128]
-            at += FINE_PAD
+            buf_ref[b, at : at + NFINE, :] = pooled[:NFINE, lo : lo + 128]
+            at += NFINE
         for t in range(half_c // 128):
             lo = b * half_c + t * 128
-            buf_ref[b, at : at + CELL_PAD, :] = weighted[:, lo : lo + 128]
-            at += CELL_PAD
+            buf_ref[b, at : at + NSENT + 1, :] = weighted[: NSENT + 1, lo : lo + 128]
+            at += NSENT + 1
+        if at < buf_ref.shape[1]:
+            buf_ref[b, at:, :] = jnp.zeros((buf_ref.shape[1] - at, 128), f32)
     keep_ref[...] = buf_ref[bit]
     send_ref[...] = buf_ref[1 - bit]
 
 
 def half_rows(width, channels):
-    return FINE_PAD * (width // 256) + CELL_PAD * (channels // 256)
+    return up(NFINE * (width // 256) + (NSENT + 1) * (channels // 256), 8)
 
 
 def direct_kernel(
@@ -466,14 +565,15 @@
     )
     upper = share.astype(bf16)
     lower = (share - upper.astype(f32)).astype(bf16)
-    lane = lax.broadcasted_iota(jnp.int32, share.shape, 1)
     share_ref[:, :128] = upper
     share_ref[:, 128:] = lower
 
 
-def two_parts(value):
-    upper = value.astype(bf16)
-    return upper, (value - upper.astype(f32)).astype(bf16)
+def two_part_dot(value, weight):
+    first = value.astype(bf16).astype(f32)
+    parts = jnp.concatenate([first, value - first], 0).astype(bf16)
+    product = contract(parts, weight, ((1,), (0,)))
+    return product[: value.shape[0]] + product[value.shape[0] :]
 
 
 def final_kernel(
@@ -501,46 +601,45 @@
     half_w, half_c = width // 2, channels // 2
     buf_ref[bit] = mine_ref[...]
     buf_ref[1 - bit] = other_ref[...]
+    pool_ref[NFINE:, :] = jnp.zeros((pool_ref.shape[0] - NFINE, width), f32)
+    wei_ref[NSENT + 1 :, :] = jnp.zeros((wei_ref.shape[0] - NSENT - 1, channels), f32)
     for b in range(2):
         at = 0
         for t in range(half_w // 128):
             lo = b * half_w + t * 128
-            pool_ref[:, lo : lo + 128] = buf_ref[b, at : at + FINE_PAD, :]
-            at += FINE_PAD
+            pool_ref[:NFINE, lo : lo + 128] = buf_ref[b, at : at + NFINE, :]
+            at += NFINE
         for t in range(half_c // 128):
             lo = b * half_c + t * 128
-            wei_ref[:, lo : lo + 128] = buf_ref[b, at : at + CELL_PAD, :]
-            at += CELL_PAD
-    cells = contract(group_ref[...], pool_ref[...], ((1,), (0,)), precision=highest)
+            wei_ref[: NSENT + 1, lo : lo + 128] = buf_ref[b, at : at + NSENT + 1, :]
+            at += NSENT + 1
+    pool = jnp.concatenate(f32_parts(pool_ref[...]), 0).astype(bf16)
+    cells = contract(group_ref[...], pool, ((1,), (0,)))
     proj_ref[...] = jnp.zeros_like(proj_ref)
     start = 0
-    for k, s in enumerate(bin_scales):
-        count = s * s
+    for k, (s, (first, count)) in enumerate(zip(bin_scales, cell_slots()[0])):
         scale = 1.0 / float((height // s) * (breadth // s))
-        upper, lower = two_parts(cells[start : start + count] * scale)
-        hidden = contract(upper, wb_ref[k], ((1,), (0,))) + contract(lower, wb_ref[k], ((1,), (0,)))
+        hidden = two_part_dot(cells[first : first + count] * scale, wb_ref[k])
         hidden = jnp.maximum(hidden + bb_ref[k : k + 1, :], 0.0)
-        upper, lower = two_parts(hidden)
-        proj_ref[start : start + count, :] = contract(upper, jb_ref[k], ((1,), (0,))) + contract(
-            lower, jb_ref[k], ((1,), (0,))
-        )
-        start += count
+        lift = two_part_dot(hidden, jb_ref[k])
+        proj_ref[start : start + s * s, :] = lift[: s * s]
+        start += s * s
     projected = proj_ref[...]
+    parts = [part.astype(bf16) for part in f32_parts(projected)]
     everyone = float(height * breadth)
-    spun = contract(gram_ref[...], projected, ((1,), (0,)), precision=highest)
+    spun = folded(contract(gram_ref[...], jnp.concatenate(parts, 0), ((1,), (0,))))
     weighted = wei_ref[...]
-    lifted_sum = spun[NCELL : NCELL + 1]
-    mixed = projected[:NCELL] * (spun[:NCELL] + 2.0 * weighted[:NCELL])
-    mean_val = (weighted[0:1] + lifted_sum) * (1.0 / everyone)
-    variance = (weighted[NCELL : NCELL + 1] + jnp.sum(mixed, 0, keepdims=True)) * (
+    which = lax.broadcasted_iota(jnp.int32, weighted.shape, 0)
+    finest = jnp.where((which >= NSENT - NFINE) & (which < NSENT), weighted, 0.0)
+    mean_val = (jnp.sum(finest, 0, keepdims=True) + spun[NCELL : NCELL + 1]) * (1.0 / everyone)
+    cross = jnp.sum(weighted * spun[64 : 64 + CELL_PAD], 0, keepdims=True)
+    square = jnp.sum(projected * spun[:64], 0, keepdims=True)
+    variance = (weighted[NSENT : NSENT + 1] + 2.0 * cross + square) * (
         1.0 / everyone
     ) - mean_val * mean_val
     scale = lax.rsqrt(variance + norm_eps) * gain_ref[...][None, :]
-    upper, lower = two_parts(projected)
-    stack = jnp.concatenate([upper, lower], 0)
-    lifted = contract(share_ref[:, :128], stack, ((1,), (0,))) + contract(
-        share_ref[:, 128:], stack, ((1,), (0,))
-    )
+    stack = jnp.concatenate(parts[:2] * 2, 0)
+    lifted = contract(share_ref[...], stack, ((1,), (0,)))
     joined = (direct_ref[...] + lifted - mean_val) * scale + bias_ref[...][None, :]
     out_ref[...] = jnp.maximum(joined, 0.0).astype(bf16)
 
@@ -589,21 +688,23 @@
     shape = jax.ShapeDtypeStruct
     own = tokens.reshape(count, width)
     send_table = roll_send(row_count, col_count)
-    send_rr, send_rc, send_rd = pl.pallas_call(
+    send_rr, send_rc, send_rd, near_rel = pl.pallas_call(
         functools.partial(send_kernel, geo),
-        out_shape=[shape((size, width), bf16) for size in sizes[1:]],
-        in_specs=[hbm] * 2,
-        out_specs=[vmem] * 3,
+        out_shape=[shape((size, width), bf16) for size in sizes[1:]]
+        + [shape(rel_table.shape, rel_table.dtype)],
+        in_specs=[hbm] * 3,
+        out_specs=[vmem] * 4,
         scratch_shapes=[
             pltpu.VMEM((count, width), bf16),
             pltpu.VMEM(send_table.shape, bf16),
-            pltpu.SemaphoreType.DMA((2,)),
+            pltpu.SemaphoreType.DMA((3,)),
         ],
         compiler_params=pltpu.CompilerParams(vmem_limit_bytes=8 << 20),
         name="send_pieces",
     )(
         pltpu.with_memory_space_constraint(own, pltpu.HBM),
         pltpu.with_memory_space_constraint(jnp.asarray(send_table, bf16), pltpu.HBM),
+        pltpu.with_memory_space_constraint(rel_table, pltpu.HBM),
     )
     rr = shifted(send_rr, -1, 0)
     rd = shifted(send_rd, -1, -1)
@@ -615,19 +716,19 @@
     grid = np.zeros((count, 8), np.float32)
     grid[:, 0] = np.arange(count) // col_count
     grid[:, 1] = np.arange(count) % col_count
-    cells = cell_table(height, breadth)
+    cells = cell_table(height, breadth, False)
+    sent_cells = cell_table(height, breadth, True)
     cell_lanes = np.zeros((8, 128), np.float32)
     cell_lanes[:, :64] = cells.T
     cell_lanes[:, 64:] = cells.T
     rows_half = half_rows(width, channels)
-    per_tile = 128 // (width // rel_table.shape[2])
 
     small = np.zeros((128, 384), np.float32)
     small[:8, :count] = token_lanes
-    small[8:72, :8] = cells
+    small[8:72, :8] = sent_cells
     small[72 : 72 + FINE_PAD, :8] = fine_table(height, breadth)
     pair_bias, near_proj, near_join, near_gather, near_scatter, near_small, near_own = expanded_bias(
-        rel_table,
+        near_rel,
         proj_weight,
         join_block,
         jnp.asarray(roll_gather(row_count, col_count), bf16),
@@ -651,12 +752,12 @@
             pltpu.VMEM((nwin, width, WIN * WIN), bf16),
             pltpu.VMEM((nwin, width, WIN * WIN), bf16),
             pltpu.VMEM((count, width), bf16),
-            pltpu.VMEM((nwin, WIN * WIN, WIN * WIN), f32),
+            pltpu.VMEM((2, nwin, WIN * WIN, 128), f32),
             pltpu.VMEM((2, rows_half, 128), f32),
-            pltpu.VMEM((per_tile, WIN * WIN, WIN * WIN), f32),
-            pltpu.VMEM((per_tile, WIN * WIN, WIN * WIN), f32),
-            pltpu.VMEM((per_tile, WIN * WIN, WIN * WIN), bf16),
-            pltpu.VMEM((per_tile, WIN * WIN, WIN * WIN), bf16),
+            pltpu.VMEM((GROUP + 1, WIN * WIN, 128), f32),
+            pltpu.VMEM((GROUP + 1, WIN * WIN, 128), f32),
+            pltpu.VMEM((GROUP + 1, WIN * WIN, 128), bf16),
+            pltpu.VMEM((GROUP + 1, WIN * WIN, 128), bf16),
         ],
         compiler_params=pltpu.CompilerParams(vmem_limit_bytes=24 << 20),
         name="window_attention",
@@ -731,8 +832,8 @@
         branch_weight,
         branch_bias,
         join_branch,
-        jnp.asarray(group_table()),
-        jnp.asarray(gram_tables(height, breadth)),
+        jnp.asarray(group_table(), bf16),
+        jnp.asarray(gram_tables(height, breadth), bf16),
         bn_gain,
         bn_bias,
     )

time: 59.6 us -> 54.9 us (0.921)
  Pallas kernels: 18.7 us -> 15.9 us
  waiting for transfers between devices: 21.4 us -> 20.1 us
  local copies, waits for them, and re-layouts: 1.05 us -> 0.09 us
    pallas_call x1, Pallas kernels: 9.14 us -> 6.53 us  [shards(): pl.pallas_call(functools.partial(attention_kernel, geo), out_shape=[shape...]
    ppermute x6, waiting for transfers between devices: 17.8 us -> 16.5 us  [exchanged(): return lax.ppermute(value, axes, [(i, i ^ mask) for i in range(everyone)])]
    unnamed x34 -> x32, local copies, waits for them, and re-layouts: 1.05 us -> 0.09 us
    pallas_call x1, Pallas kernels: 3.29 us -> 2.49 us  [shards(): pl.pallas_call(functools.partial(final_kernel, geo), out_shape=shape((cou...]
  transfers between devices with their start and end apart: 12 -> 12, of which waited for: 6 -> 6; matrix products, arithmetic and copies ran while one was open for 0% -> 0% of each run, Pallas kernels for 8% -> 9%
where the time goes in v1:
time: 54.9 us; the launch traced here: 54.8 us
  waiting for transfers between devices  20.1 us (37%)
  starting transfers between devices  18.3 us (33%)
  Pallas kernels  15.9 us (29%)
    ppermute x6, waiting for transfers between devices, exchanged(): return lax.ppermute(value, axes, [(i, i ^ mask) for i in range(everyone)])  16.5 us
    ppermute x6, starting transfers between devices, shifted(): return lax.ppermute(value, axes, pairs)  14.2 us
    pallas_call x1, Pallas kernels, shards(): pl.pallas_call(functools.partial(attention_kernel, geo), out_shape=[shape...  6.53 us
    pallas_call x1, Pallas kernels, expanded_bias(): pl.pallas_call(functools.partial(bias_kernel, len(brought)), out_shape=[j...  4.56 us
    ppermute x6, starting transfers between devices, exchanged(): return lax.ppermute(value, axes, [(i, i ^ mask) for i in range(everyone)])  4.12 us
    ppermute x6, waiting for transfers between devices, shifted(): return lax.ppermute(value, axes, pairs)  3.62 us
    pallas_call x1, Pallas kernels, shards(): pl.pallas_call(functools.partial(final_kernel, geo), out_shape=shape((cou...  2.49 us
    pallas_call x1, Pallas kernels, shards(): pl.pallas_call(functools.partial(send_kernel, geo), out_shape=[shape((siz...  1.66 us
  transfers between devices with their start and end apart: 12, of which 6 were waited for; matrix products, arithmetic and copies ran while one was open for 0% of the time, Pallas kernels for 9%

profile of v1, /device:TPU:0, one launch (start us, length us, event | category | flops | bytes accessed | tf_op | source)
XLA Modules:
  0.0 54.8 jit_solution(4836661610804500087)
XLA Ops:
  0.0 1.7 %send_pieces.1 = (bf16[108,768]{1,0:T(8,128)(2,1)S(1)}, bf16[36,768]{1,0:T(8,128)(2,1)S(1)}, bf16[36,768]{1,0:T(8,128)(2,1)S(1)}, f32[23,23,24]{2,1,0:T(8,128)S(1)}) custom-call(bf16[288,768]{1,0:T(8,128)(2,1)} %bitcast.2, bf16[208,288]{1,0:T(8,128)(2,1)} %constant.18.clone.table_ref, f32[23,23,24]{2,1,0:T(8,128)} %rel_ref.1), custom_call_target="tpu_custom_call" | custom-call | tf_op jit(solution)/shard_map/send_pieces/pallas_call | solution.py:691
  1.7 6.1 %collective-permute-start = (bf16[108,768]{1,0:T(8,128)(2,1)S(1)}, bf16[108,768]{1,0:T(8,128)(2,1)S(1)}, u32[]{:S(2)}, u32[]{:S(2)}) collective-permute-start(bf16[108,768]{1,0:T(8,128)(2,1)S(1)} %get-tuple-element.26), channel_id=1, source_target_pairs={{0,28},{1,29},{2,30},{3,31},{4,0},{5,1},{6,2},{7,3},{8,4},{9,5},{1... | collective-permute-start | bytes 497672 | tf_op jit(solution)/shard_map/ppermute | solution.py:680
  7.8 0.7 %collective-permute-start.1 = (bf16[36,768]{1,0:T(8,128)(2,1)S(1)}, bf16[36,768]{1,0:T(8,128)(2,1)S(1)}, u32[]{:S(2)}, u32[]{:S(2)}) collective-permute-start(bf16[36,768]{1,0:T(8,128)(2,1)S(1)} %get-tuple-element.27), channel_id=1, source_target_pairs={{0,3},{1,0},{2,1},{3,2},{4,7},{5,4},{6,5},{7,6},{8,11},{9,8},{10,9... | collective-permute-start | bytes 165896 | tf_op jit(solution)/shard_map/ppermute | solution.py:680
  8.4 0.9 %collective-permute-start.2 = (bf16[36,768]{1,0:T(8,128)(2,1)S(1)}, bf16[36,768]{1,0:T(8,128)(2,1)S(1)}, u32[]{:S(2)}, u32[]{:S(2)}) collective-permute-start(bf16[36,768]{1,0:T(8,128)(2,1)S(1)} %get-tuple-element.28), channel_id=1, source_target_pairs={{0,31},{1,28},{2,29},{3,30},{4,3},{5,0},{6,1},{7,2},{8,7},{9,4},{1... | collective-permute-start | bytes 165896 | tf_op jit(solution)/shard_map/ppermute | solution.py:680
  9.3 4.6 %expand_bias.1 = (f32[27,144,128]{2,1,0:T(8,128)S(1)}, bf16[768,768]{1,0:T(8,128)(2,1)S(1)}, bf16[768,512]{1,0:T(8,128)(2,1)S(1)}, bf16[288,496]{1,0:T(8,128)(2,...) custom-call(f32[23,23,24]{2,1,0:T(8,128)S(1)} %get-tuple-element.24.table_ref, ...), custom_call_target="tpu_custom_call" | custom-call | flops 1990656 | bytes 1990656 | tf_op jit(solution)/shard_map/expand_bias/pallas_call | solution.py:317
  14.0 0.0 copy-start.2
  14.0 0.0 copy-start.4
  14.0 0.0 copy-start.6
  14.0 0.0 copy-start.13
  14.0 0.0 copy-start.3
  14.0 0.0 copy-start.5
  14.1 6.5 %window_attention.1 = (f32[200,128]{1,0:T(8,128)S(1)}, f32[200,128]{1,0:T(8,128)S(1)}, bf16[108,768]{1,0:T(8,128)(2,1)S(1)}, bf16[108,768]{1,0:T(8,128)(2,1)S(1)...) custom-call(bf16[288,768]{1,0:T(8,128)(2,1)S(1)} %get-tuple-element.25.own_ref, ...), custom_call_target="tpu_custom_call" | custom-call | tf_op jit(solution)/shard_map/window_attention/pallas_call | solution.py:739
  20.6 0.0 copy-start.1
  20.6 0.0 copy-start.7
  20.6 0.0 copy-start.9
  20.6 0.1 collective-permute-start.3
  20.7 1.3 %collective-permute-done.3 = f32[200,128]{1,0:T(8,128)S(1)} collective-permute-done((f32[200,128]{1,0:T(8,128)S(1)}, f32[200,128]{1,0:T(8,128)S(1)}, u32[]{:S(2)}, u32[]{:S(2)}) %collective-permute-start.3) | collective-permute-done | bytes 102432 | tf_op jit(solution)/shard_map/ppermute | solution.py:683
  22.0 0.6 %collective-permute-start.4 = (f32[200,128]{1,0:T(8,128)S(1)}, f32[200,128]{1,0:T(8,128)S(1)}, u32[]{:S(2)}, u32[]{:S(2)}) collective-permute-start(f32[200,128]{1,0:T(8,128)S(1)} %add.15), channel_id=1, source_target_pairs={{0,2},{1,3},{2,0},{3,1},{4,6},{5,7},{6,4},{7,5},{8,10},{9,11},{10,... | collective-permute-start | bytes 307208 | tf_op jit(solution)/shard_map/ppermute | solution.py:683
  22.6 4.4 %collective-permute-done.4 = f32[200,128]{1,0:T(8,128)S(1)} collective-permute-done((f32[200,128]{1,0:T(8,128)S(1)}, f32[200,128]{1,0:T(8,128)S(1)}, u32[]{:S(2)}, u32[]{:S(2)}) %collective-permute-start.4) | collective-permute-done | bytes 102432 | tf_op jit(solution)/shard_map/ppermute | solution.py:683
  27.1 1.6 %collective-permute-start.5 = (f32[200,128]{1,0:T(8,128)S(1)}, f32[200,128]{1,0:T(8,128)S(1)}, u32[]{:S(2)}, u32[]{:S(2)}) collective-permute-start(f32[200,128]{1,0:T(8,128)S(1)} %add.16), channel_id=1, source_target_pairs={{0,4},{1,5},{2,6},{3,7},{4,0},{5,1},{6,2},{7,3},{8,12},{9,13},{10,... | collective-permute-start | bytes 307208 | tf_op jit(solution)/shard_map/ppermute | solution.py:683
  28.6 3.1 %collective-permute-done.5 = f32[200,128]{1,0:T(8,128)S(1)} collective-permute-done((f32[200,128]{1,0:T(8,128)S(1)}, f32[200,128]{1,0:T(8,128)S(1)}, u32[]{:S(2)}, u32[]{:S(2)}) %collective-permute-start.5) | collective-permute-done | bytes 102432 | tf_op jit(solution)/shard_map/ppermute | solution.py:683
  31.8 0.1 collective-permute-start.6
  31.9 4.6 %collective-permute-done.6 = f32[200,128]{1,0:T(8,128)S(1)} collective-permute-done((f32[200,128]{1,0:T(8,128)S(1)}, f32[200,128]{1,0:T(8,128)S(1)}, u32[]{:S(2)}, u32[]{:S(2)}) %collective-permute-start.6) | collective-permute-done | bytes 102432 | tf_op jit(solution)/shard_map/ppermute | solution.py:683
  36.5 1.7 %collective-permute-start.7 = (f32[200,128]{1,0:T(8,128)S(1)}, f32[200,128]{1,0:T(8,128)S(1)}, u32[]{:S(2)}, u32[]{:S(2)}) collective-permute-start(f32[200,128]{1,0:T(8,128)S(1)} %add.18), channel_id=1, source_target_pairs={{0,16},{1,17},{2,18},{3,19},{4,20},{5,21},{6,22},{7,23},{8,24},{9,... | collective-permute-start | bytes 307208 | tf_op jit(solution)/shard_map/ppermute | solution.py:683
  38.3 2.0 %collective-permute-start.9 = (bf16[108,768]{1,0:T(8,128)(2,1)S(1)}, bf16[108,768]{1,0:T(8,128)(2,1)S(1)}, u32[]{:S(2)}, u32[]{:S(2)}) collective-permute-start(bf16[108,768]{1,0:T(8,128)(2,1)S(1)} %get-tuple-element.38), channel_id=1, source_target_pairs={{0,4},{1,5},{2,6},{3,7},{4,8},{5,9},{6,10},{7,11},{8,12},{9,13},{1... | collective-permute-start | bytes 497672 | tf_op jit(solution)/shard_map/ppermute | solution.py:680
  40.3 3.0 %collective-permute-done.7 = f32[200,128]{1,0:T(8,128)S(1)} collective-permute-done((f32[200,128]{1,0:T(8,128)S(1)}, f32[200,128]{1,0:T(8,128)S(1)}, u32[]{:S(2)}, u32[]{:S(2)}) %collective-permute-start.7) | collective-permute-done | bytes 102432 | tf_op jit(solution)/shard_map/ppermute | solution.py:683
  43.3 0.1 collective-permute-start.8
  43.4 0.5 collective-permute-start.10
  43.9 4.1 %collective-permute-start.11 = (bf16[36,768]{1,0:T(8,128)(2,1)S(1)}, bf16[36,768]{1,0:T(8,128)(2,1)S(1)}, u32[]{:S(2)}, u32[]{:S(2)}) collective-permute-start(bf16[36,768]{1,0:T(8,128)(2,1)S(1)} %get-tuple-element.40), channel_id=1, source_target_pairs={{0,5},{1,6},{2,7},{3,4},{4,9},{5,10},{6,11},{7,8},{8,13},{9,14},{1... | collective-permute-start | bytes 165896 | tf_op jit(solution)/shard_map/ppermute | solution.py:680
  47.9 3.6 %collective-permute-done.11.rd_ref = bf16[36,768]{1,0:T(8,128)(2,1)S(1)} collective-permute-done((bf16[36,768]{1,0:T(8,128)(2,1)S(1)}, bf16[36,768]{1,0:T(8,128)(2,1)S(1)}, u32[]{:S(2)}, u32[]{:S(2)}) %collective-permute-start.11) | collective-permute-done | bytes 55328 | tf_op jit(solution)/shard_map/ppermute | solution.py:680
  51.6 0.6 %direct_join.1 = (f32[288,512]{1,0:T(8,128)S(1)}, bf16[288,256]{1,0:T(8,128)(2,1)S(1)}) custom-call(bf16[108,768]{1,0:T(8,128)(2,1)S(1)} %get-tuple-element.37.own_ref, bf16[108,768]{1,0:T(8,128)(2,1)S(1)} %collective-permute-done.9.rr_ref, bf16[36,768]{1,0:T(8,128)(2,1)S(1)} %collective-permute-done.10.rc_ref, ...), custom_call_target="tpu_custom_call" | custom-call | flops 226492416 | bytes 4194304 | tf_op jit(solution)/shard_map/direct_join/pallas_call | solution.py:792
  52.3 2.5 %final_join.1 = bf16[288,512]{1,0:T(8,128)(2,1)} custom-call(f32[200,128]{1,0:T(8,128)S(1)} %add.19.mine_ref, f32[200,128]{1,0:T(8,128)S(1)} %collective-permute-done.8.other_ref, f32[288,512]{1,0:T(8,128)S(1)} %get-tuple-element.41.direct_ref, bf16[288,256]{1,0:T(8,128)(2,1)S(1)} %get-tuple-element.42.share_ref, bf16[4,768,512]{2,1,0:T(8,128)(2,1)S(1)} %copy-done.1, ...), custom_call_target="tpu_custom_call" | custom-call | tf_op jit(solution)/shard_map/final_join/pallas_call | solution.py:814
  (34 shorter events, 0.1 us)
Async XLA Ops:
  0.0 13.9 %copy-start = (bf16[768,2304]{1,0:T(8,128)(2,1)S(1)}, bf16[768,2304]{1,0:T(8,128)(2,1)}, u32[]{:S(2)}) copy-start(bf16[768,2304]{1,0:T(8,128)(2,1)} %wqkv_ref.1) | copy-start | bytes 10616836
  0.0 13.9 %copy-start.8 = (f32[2304]{0:T(1024)S(1)}, f32[2304]{0:T(1024)}, u32[]{:S(2)}) copy-start(f32[2304]{0:T(1024)} %bqkv_ref.1) | copy-start | bytes 27652
  0.0 13.9 %copy-start.10 = (f32[768]{0:T(1024)S(1)}, f32[768]{0:T(1024)}, u32[]{:S(2)}) copy-start(f32[768]{0:T(1024)} %lng_ref.1) | copy-start | bytes 9220
  0.0 14.0 %copy-start.11 = (f32[768]{0:T(1024)S(1)}, f32[768]{0:T(1024)}, u32[]{:S(2)}) copy-start(f32[768]{0:T(1024)} %lnb_ref.1) | copy-start | bytes 9220
  0.0 14.0 %copy-start.12 = (f32[768]{0:T(1024)S(1)}, f32[768]{0:T(1024)}, u32[]{:S(2)}) copy-start(f32[768]{0:T(1024)} %bproj_ref.1) | copy-start | bytes 9220
  1.7 12.2 %collective-permute-start = (bf16[108,768]{1,0:T(8,128)(2,1)S(1)}, bf16[108,768]{1,0:T(8,128)(2,1)S(1)}, u32[]{:S(2)}, u32[]{:S(2)}) collective-permute-start(bf16[108,768]{1,0:T(8,128)(2,1)S(1)} %get-tuple-element.26), channel_id=1, source_target_pairs={{0,28},{1,29},{2,30},{3,31},{4,0},{5,1},{6,2},{7,3},{8,4},{9,5},{1... | collective-permute-start | bytes 497672 | tf_op jit(solution)/shard_map/ppermute | solution.py:680
  7.8 6.1 %collective-permute-start.1 = (bf16[36,768]{1,0:T(8,128)(2,1)S(1)}, bf16[36,768]{1,0:T(8,128)(2,1)S(1)}, u32[]{:S(2)}, u32[]{:S(2)}) collective-permute-start(bf16[36,768]{1,0:T(8,128)(2,1)S(1)} %get-tuple-element.27), channel_id=1, source_target_pairs={{0,3},{1,0},{2,1},{3,2},{4,7},{5,4},{6,5},{7,6},{8,11},{9,8},{10,9... | collective-permute-start | bytes 165896 | tf_op jit(solution)/shard_map/ppermute | solution.py:680
  8.4 5.5 %collective-permute-start.2 = (bf16[36,768]{1,0:T(8,128)(2,1)S(1)}, bf16[36,768]{1,0:T(8,128)(2,1)S(1)}, u32[]{:S(2)}, u32[]{:S(2)}) collective-permute-start(bf16[36,768]{1,0:T(8,128)(2,1)S(1)} %get-tuple-element.28), channel_id=1, source_target_pairs={{0,31},{1,28},{2,29},{3,30},{4,3},{5,0},{6,1},{7,2},{8,7},{9,4},{1... | collective-permute-start | bytes 165896 | tf_op jit(solution)/shard_map/ppermute | solution.py:680
  14.0 37.6 %copy-start.2 = (bf16[768,512]{1,0:T(8,128)(2,1)S(1)}, bf16[768,512]{1,0:T(8,128)(2,1)}, u32[]{:S(2)}) copy-start(bf16[768,512]{1,0:T(8,128)(2,1)} %wjoin_ref.1) | copy-start | bytes 2359300
  14.0 37.5 %copy-start.4 = (bf16[288,320]{1,0:T(8,128)(2,1)S(1)}, bf16[288,320]{1,0:T(8,128)(2,1)}, u32[]{:S(2)}) copy-start(bf16[288,320]{1,0:T(8,128)(2,1)} %constant.22.clone.gather_ref) | copy-start | bytes 552964
  14.0 37.5 %copy-start.6 = (f32[288,8]{1,0:T(8,128)S(1)}, f32[288,8]{1,0:T(8,128)}, u32[]{:S(2)}) copy-start(f32[288,8]{1,0:T(8,128)} %constant.23.clone.token_ref) | copy-start | bytes 27652
  14.0 37.5 %copy-start.13 = (f32[8,128]{1,0:T(8,128)S(1)}, f32[8,128]{1,0:T(8,128)}, u32[]{:S(2)}) copy-start(f32[8,128]{1,0:T(8,128)} %constant.24.clone.cell_ref) | copy-start | bytes 12292
  14.0 38.2 %copy-start.3 = (bf16[4,512,512]{2,1,0:T(8,128)(2,1)S(1)}, bf16[4,512,512]{2,1,0:T(8,128)(2,1)}, u32[]{:S(2)}) copy-start(bf16[4,512,512]{2,1,0:T(8,128)(2,1)} %jb_ref.1) | copy-start | bytes 6291460
  14.0 38.2 %copy-start.5 = (bf16[336,192]{1,0:T(8,128)(2,1)S(1)}, bf16[336,192]{1,0:T(8,128)(2,1)}, u32[]{:S(2)}) copy-start(bf16[336,192]{1,0:T(8,128)(2,1)} %constant.26.clone.gram_ref) | copy-start | bytes 387076
  20.6 31.6 %copy-start.1 = (bf16[4,768,512]{2,1,0:T(8,128)(2,1)S(1)}, bf16[4,768,512]{2,1,0:T(8,128)(2,1)}, u32[]{:S(2)}) copy-start(bf16[4,768,512]{2,1,0:T(8,128)(2,1)} %wb_ref.1) | copy-start | bytes 9437188
  20.6 31.6 %copy-start.7 = (bf16[72,120]{1,0:T(8,128)(2,1)S(1)}, bf16[72,120]{1,0:T(8,128)(2,1)}, u32[]{:S(2)}) copy-start(bf16[72,120]{1,0:T(8,128)(2,1)} %constant.25.clone.group_ref) | copy-start | bytes 51844
  20.6 31.6 %copy-start.9 = (f32[4,512]{1,0:T(4,128)S(1)}, f32[4,512]{1,0:T(4,128)}, u32[]{:S(2)}) copy-start(f32[4,512]{1,0:T(4,128)} %bb_ref.1) | copy-start | bytes 24580
  20.6 31.6 %copy-start.14 = (f32[512]{0:T(512)S(1)}, f32[512]{0:T(512)}, u32[]{:S(2)}) copy-start(f32[512]{0:T(512)} %gain_ref.1) | copy-start | bytes 6148
  20.6 31.6 %copy-start.15 = (f32[512]{0:T(512)S(1)}, f32[512]{0:T(512)}, u32[]{:S(2)}) copy-start(f32[512]{0:T(512)} %bias_ref.1) | copy-start | bytes 6148
  20.6 1.4 %collective-permute-start.3 = (f32[200,128]{1,0:T(8,128)S(1)}, f32[200,128]{1,0:T(8,128)S(1)}, u32[]{:S(2)}, u32[]{:S(2)}) collective-permute-start(f32[200,128]{1,0:T(8,128)S(1)} %get-tuple-element.36), channel_id=1, source_target_pairs={{0,1},{1,0},{2,3},{3,2},{4,5},{5,4},{6,7},{7,6},{8,9},{9,8},{10,11... | collective-permute-start | bytes 307208 | tf_op jit(solution)/shard_map/ppermute | solution.py:683
  22.0 5.0 %collective-permute-start.4 = (f32[200,128]{1,0:T(8,128)S(1)}, f32[200,128]{1,0:T(8,128)S(1)}, u32[]{:S(2)}, u32[]{:S(2)}) collective-permute-start(f32[200,128]{1,0:T(8,128)S(1)} %add.15), channel_id=1, source_target_pairs={{0,2},{1,3},{2,0},{3,1},{4,6},{5,7},{6,4},{7,5},{8,10},{9,11},{10,... | collective-permute-start | bytes 307208 | tf_op jit(solution)/shard_map/ppermute | solution.py:683
  27.1 4.7 %collective-permute-start.5 = (f32[200,128]{1,0:T(8,128)S(1)}, f32[200,128]{1,0:T(8,128)S(1)}, u32[]{:S(2)}, u32[]{:S(2)}) collective-permute-start(f32[200,128]{1,0:T(8,128)S(1)} %add.16), channel_id=1, source_target_pairs={{0,4},{1,5},{2,6},{3,7},{4,0},{5,1},{6,2},{7,3},{8,12},{9,13},{10,... | collective-permute-start | bytes 307208 | tf_op jit(solution)/shard_map/ppermute | solution.py:683
  31.8 4.7 %collective-permute-start.6 = (f32[200,128]{1,0:T(8,128)S(1)}, f32[200,128]{1,0:T(8,128)S(1)}, u32[]{:S(2)}, u32[]{:S(2)}) collective-permute-start(f32[200,128]{1,0:T(8,128)S(1)} %add.17), channel_id=1, source_target_pairs={{0,8},{1,9},{2,10},{3,11},{4,12},{5,13},{6,14},{7,15},{8,0},{9,1},... | collective-permute-start | bytes 307208 | tf_op jit(solution)/shard_map/ppermute | solution.py:683
  36.5 6.7 %collective-permute-start.7 = (f32[200,128]{1,0:T(8,128)S(1)}, f32[200,128]{1,0:T(8,128)S(1)}, u32[]{:S(2)}, u32[]{:S(2)}) collective-permute-start(f32[200,128]{1,0:T(8,128)S(1)} %add.18), channel_id=1, source_target_pairs={{0,16},{1,17},{2,18},{3,19},{4,20},{5,21},{6,22},{7,23},{8,24},{9,... | collective-permute-start | bytes 307208 | tf_op jit(solution)/shard_map/ppermute | solution.py:683
  38.3 13.3 %collective-permute-start.9 = (bf16[108,768]{1,0:T(8,128)(2,1)S(1)}, bf16[108,768]{1,0:T(8,128)(2,1)S(1)}, u32[]{:S(2)}, u32[]{:S(2)}) collective-permute-start(bf16[108,768]{1,0:T(8,128)(2,1)S(1)} %get-tuple-element.38), channel_id=1, source_target_pairs={{0,4},{1,5},{2,6},{3,7},{4,8},{5,9},{6,10},{7,11},{8,12},{9,13},{1... | collective-permute-start | bytes 497672 | tf_op jit(solution)/shard_map/ppermute | solution.py:680
  43.3 8.9 %collective-permute-start.8 = (f32[200,128]{1,0:T(8,128)S(1)}, f32[200,128]{1,0:T(8,128)S(1)}, u32[]{:S(2)}, u32[]{:S(2)}) collective-permute-start(f32[200,128]{1,0:T(8,128)S(1)} %add.19.mine_ref), channel_id=1, source_target_pairs={{0,1},{1,0},{2,3},{3,2},{4,5},{5,4},{6,7},{7,6},{8,9},{9,8},{10,11... | collective-permute-start | bytes 307208 | tf_op jit(solution)/shard_map/ppermute | solution.py:683
  43.4 4.6 %collective-permute-start.10 = (bf16[36,768]{1,0:T(8,128)(2,1)S(1)}, bf16[36,768]{1,0:T(8,128)(2,1)S(1)}, u32[]{:S(2)}, u32[]{:S(2)}) collective-permute-start(bf16[36,768]{1,0:T(8,128)(2,1)S(1)} %get-tuple-element.39), channel_id=1, source_target_pairs={{0,1},{1,2},{2,3},{3,0},{4,5},{5,6},{6,7},{7,4},{8,9},{9,10},{10,1... | collective-permute-start | bytes 165896 | tf_op jit(solution)/shard_map/ppermute | solution.py:680
  43.9 7.7 %collective-permute-start.11 = (bf16[36,768]{1,0:T(8,128)(2,1)S(1)}, bf16[36,768]{1,0:T(8,128)(2,1)S(1)}, u32[]{:S(2)}, u32[]{:S(2)}) collective-permute-start(bf16[36,768]{1,0:T(8,128)(2,1)S(1)} %get-tuple-element.40), channel_id=1, source_target_pairs={{0,5},{1,6},{2,7},{3,4},{4,9},{5,10},{6,11},{7,8},{8,13},{9,14},{1... | collective-permute-start | bytes 165896 | tf_op jit(solution)/shard_map/ppermute | solution.py:680

commit v2 on v1

--- a/solution.py
+++ b/solution.py
@@ -60,12 +60,13 @@
     table = np.zeros((total - base, row_count * col_count), np.float32)
     for i in range(row_count):
         for j in range(col_count):
-            if i < HALF and j >= HALF:
-                target = starts[1] + i * inner_c + (j - HALF)
-            elif i < HALF:
-                target = starts[3] + i * HALF + j
+            low = i - (row_count - HALF)
+            if low >= 0 and j >= HALF:
+                target = starts[1] + low * inner_c + (j - HALF)
+            elif low >= 0:
+                target = starts[3] + low * HALF + j
             elif j < HALF:
-                target = starts[2] + (i - HALF) * HALF + j
+                target = starts[2] + i * HALF + j
             else:
                 continue
             table[target - base, i * col_count + j] = 1.0
@@ -73,53 +74,53 @@
 
 
 def roll_gather(row_count, col_count):
-    inner_r, inner_c = row_count - HALF, col_count - HALF
+    inner_c = col_count - HALF
     _, starts, total = tile_sizes(row_count, col_count)
     table = np.zeros((row_count * col_count, total), np.float32)
     for token, (i, j) in enumerate(window_order(row_count, col_count)):
-        if i < inner_r and j < inner_c:
-            source = starts[0] + (i + HALF) * col_count + (j + HALF)
+        if i >= HALF and j < inner_c:
+            source = starts[0] + (i - HALF) * col_count + (j + HALF)
         elif j < inner_c:
-            source = starts[1] + (i - inner_r) * inner_c + j
-        elif i < inner_r:
-            source = starts[2] + i * HALF + (j - inner_c)
+            source = starts[1] + i * inner_c + j
+        elif i >= HALF:
+            source = starts[2] + (i - HALF) * HALF + (j - inner_c)
         else:
-            source = starts[3] + (i - inner_r) * HALF + (j - inner_c)
+            source = starts[3] + i * HALF + (j - inner_c)
         table[token, source] = 1.0
     return table
 
 
 def unroll_scatter(row_count, col_count):
-    inner_r, inner_c = row_count - HALF, col_count - HALF
+    inner_c = col_count - HALF
     _, starts, total = piece_sizes(row_count, col_count)
     table = np.zeros((total, row_count * col_count), np.float32)
     for token, (i, j) in enumerate(window_order(row_count, col_count)):
-        if i < inner_r and j < inner_c:
-            target = starts[0] + i * inner_c + j
+        if i >= HALF and j < inner_c:
+            target = starts[0] + (i - HALF) * inner_c + j
         elif j < inner_c:
-            target = starts[1] + (i - inner_r) * inner_c + j
-        elif i < inner_r:
-            target = starts[2] + i * HALF + (j - inner_c)
+            target = starts[1] + i * inner_c + j
+        elif i >= HALF:
+            target = starts[2] + (i - HALF) * HALF + (j - inner_c)
         else:
-            target = starts[3] + (i - inner_r) * HALF + (j - inner_c)
+            target = starts[3] + i * HALF + (j - inner_c)
         table[target, token] = 1.0
     return table
 
 
 def unroll_gather(row_count, col_count):
-    inner_c = col_count - HALF
+    inner_r, inner_c = row_count - HALF, col_count - HALF
     _, starts, total = piece_sizes(row_count, col_count)
     table = np.zeros((row_count * col_count, total), np.float32)
     for i in range(row_count):
         for j in range(col_count):
-            if i >= HALF and j >= HALF:
-                source = starts[0] + (i - HALF) * inner_c + (j - HALF)
+            if i < inner_r and j >= HALF:
+                source = starts[0] + i * inner_c + (j - HALF)
             elif j >= HALF:
-                source = starts[1] + i * inner_c + (j - HALF)
-            elif i >= HALF:
-                source = starts[2] + (i - HALF) * HALF + j
+                source = starts[1] + (i - inner_r) * inner_c + (j - HALF)
+            elif i < inner_r:
+                source = starts[2] + i * HALF + j
             else:
-                source = starts[3] + i * HALF + j
+                source = starts[3] + (i - inner_r) * HALF + j
             table[i * col_count + j, source] = 1.0
     return table
 
@@ -273,39 +274,54 @@
     sub = lax.broadcasted_iota(jnp.int32, (8, 128), 0)
     tail = WIN * WIN - 128
     per_slot = 128 // tail
-    for k in range(WIN * WIN // 8):
+    blocks = WIN * WIN // 8
+
+    def move(k):
         base = WIN * WIN - 8 - 8 * k
         tile, rest = base // 128, base % 128
-        moved = []
-        for par in range(2):
-            rolled = [
+        last = tile + 3 if rest + 7 + tail > 128 else tile + 2
+        return [
+            [
                 pltpu.roll(wide[par][t], 121 - rest, 2, stride=1, stride_axis=1)
-                for t in range(tile, min(tile + 3, 3))
+                for t in range(tile, last)
             ]
-            near = lane < 121 - rest + sub
-            first = jnp.where(near[None], rolled[0], rolled[1])
-            second = rolled[1]
-            if rest + 7 + tail > 128:
-                second = jnp.where(near[None], rolled[1], rolled[2])
-            moved.append((first, second))
+            for par in range(2)
+        ]
+
+    def choose(k, moved):
+        near = (lane < 121 - (WIN * WIN - 8 - 8 * k) % 128 + sub)[None]
         u = (8 * k + sub) // WIN
         rows = slice(8 * k, 8 * k + 8)
-        for half in range(2):
-            odd = ((128 * half + lane) // WIN + u) % 2 == 1
-            result = jnp.where(odd[None], moved[0][half], moved[1][half])
-            for g in range(heads // per_slot):
-                part = result[g * per_slot : (g + 1) * per_slot]
-                slot = g * (per_slot + 1)
-                if half == 0:
-                    out_ref[slot : slot + per_slot, rows, :] = part
-                    continue
-                part = jnp.where((lane < tail)[None], part, 0.0)
-                pieces = [part[0]] + [
-                    pltpu.roll(part[h], tail * h, 1) for h in range(1, per_slot)
-                ]
-                while len(pieces) > 1:
-                    pieces = [x + y for x, y in zip(pieces[::2], pieces[1::2])]
-                out_ref[slot + per_slot, rows, :] = pieces[0]
+        odd = ((lane // WIN + u) % 2 == 1)[None]
+        main = jnp.where(
+            odd, jnp.where(near, *moved[0][:2]), jnp.where(near, *moved[1][:2])
+        )
+        rest = [m[1] if len(m) == 2 else jnp.where(near, *m[1:]) for m in moved]
+        odd = (((128 + lane) // WIN + u) % 2 == 1)[None]
+        part = jnp.where((lane < tail)[None], jnp.where(odd, *rest), 0.0)
+        for g in range(heads // per_slot):
+            slot = g * (per_slot + 1)
+            out_ref[slot : slot + per_slot, rows, :] = main[g * per_slot : (g + 1) * per_slot]
+        return [
+            part[h] if h % per_slot == 0 else pltpu.roll(part[h], tail * (h % per_slot), 1)
+            for h in range(heads)
+        ]
+
+    def join(k, pieces):
+        for g in range(heads // per_slot):
+            mine = pieces[g * per_slot : (g + 1) * per_slot]
+            while len(mine) > 1:
+                mine = [x + y for x, y in zip(mine[::2], mine[1::2])]
+            out_ref[g * (per_slot + 1) + per_slot, 8 * k : 8 * k + 8, :] = mine[0]
+
+    moved, pieces = {}, {}
+    for k in range(blocks + 2):
+        if k < blocks:
+            moved[k] = move(k)
+        if 0 <= k - 1 < blocks:
+            pieces[k - 1] = choose(k - 1, moved.pop(k - 1))
+        if 0 <= k - 2:
+            join(k - 2, pieces.pop(k - 2))
     for copy in copies:
         copy.wait()
 
@@ -357,15 +373,15 @@
     rc_ref,
     rd_ref,
     gather_ref,
-    scatter_ref,
+    far_scatter_ref,
     lng_ref,
     lnb_ref,
     wqkv_ref,
     bqkv_ref,
     bias_ref,
-    wproj_ref,
+    far_proj_ref,
     bproj_ref,
-    wjoin_ref,
+    far_join_ref,
     small_ref,
     keep_ref,
     send_ref,
@@ -385,7 +401,18 @@
     sb_ref,
     pa_ref,
     pb_ref,
+    wproj_ref,
+    wjoin_ref,
+    scatter_ref,
+    sem,
 ):
+    copies = [
+        pltpu.make_async_copy(far_proj_ref, wproj_ref, sem.at[0]),
+        pltpu.make_async_copy(far_join_ref, wjoin_ref, sem.at[1]),
+        pltpu.make_async_copy(far_scatter_ref, scatter_ref, sem.at[2]),
+    ]
+    for copy in copies:
+        copy.start()
     row_count, col_count, height, breadth = geo
     nwr, nwc = row_count // WIN, col_count // WIN
     tokens, width = row_count * col_count, own_ref.shape[1]
@@ -424,7 +451,7 @@
         col_diff = (sub % WIN < HALF) != (query % WIN < HALF)
         for wr in range(nwr):
             for wc in range(nwc):
-                row_last = my_row * nwr + wr == height // WIN - 1
+                row_last = my_row * nwr + wr == 0
                 col_last = my_col * nwc + wc == breadth // WIN - 1
                 bad = (row_diff & row_last) | (col_diff & col_last)
                 pen_ref[kind, wr * nwc + wc] = jnp.where(bad, -100.0, 0.0)
@@ -489,6 +516,8 @@
     lax.fori_loop(0, steps // 2, step_pair, 0)
     make_context(steps - 1, pb_ref)
 
+    for copy in copies:
+        copy.wait()
     for w in range(nwr * nwc):
         attended = contract(ct_ref[w], wproj_ref[...], ((0,), (0,))) + bproj_ref[...][None, :]
         here = slice(w * wt, (w + 1) * wt)
@@ -499,9 +528,9 @@
     for ref, start, size in zip((o_own_ref, o_row_ref, o_col_ref, o_diag_ref), starts, sizes):
         ref[...] = pieces[start : start + size]
 
-    row = small_ref[0:1, :tokens] + (my_row * row_count + HALF).astype(f32)
+    row = small_ref[0:1, :tokens] + (my_row * row_count - HALF).astype(f32)
     col = small_ref[1:2, :tokens] + (my_col * col_count + HALF).astype(f32)
-    row = jnp.where(row >= height, row - height, row)
+    row = jnp.where(row < 0, row + height, row)
     col = jnp.where(col >= breadth, col - breadth, col)
     fine = small_ref[72 : 72 + FINE_PAD, :8]
     inside = (
@@ -679,8 +708,8 @@
                 )
         return lax.ppermute(value, axes, pairs)
 
-    def exchanged(value, mask):
-        return lax.ppermute(value, axes, [(i, i ^ mask) for i in range(everyone)])
+    def exchanged(value, masks):
+        return lax.ppermute(value, axes, [(i, i ^ masks[i % 2]) for i in range(everyone)])
 
     vmem = pl.BlockSpec(memory_space=pltpu.VMEM)
     hbm = pl.BlockSpec(memory_space=pltpu.HBM)
@@ -706,8 +735,8 @@
         pltpu.with_memory_space_constraint(jnp.asarray(send_table, bf16), pltpu.HBM),
         pltpu.with_memory_space_constraint(rel_table, pltpu.HBM),
     )
-    rr = shifted(send_rr, -1, 0)
-    rd = shifted(send_rd, -1, -1)
+    rr = shifted(send_rr, 1, 0)
+    rd = shifted(send_rd, 1, -1)
     rc = shifted(send_rc, 0, -1)
 
     order = np.array(window_order(row_count, col_count), np.float32)
@@ -727,15 +756,14 @@
     small[:8, :count] = token_lanes
     small[8:72, :8] = sent_cells
     small[72 : 72 + FINE_PAD, :8] = fine_table(height, breadth)
-    pair_bias, near_proj, near_join, near_gather, near_scatter, near_small, near_own = expanded_bias(
+    pair_bias, near_qkv, near_gather, near_small, near_own = expanded_bias(
         near_rel,
-        proj_weight,
-        join_block,
+        qkv_weight,
         jnp.asarray(roll_gather(row_count, col_count), bf16),
-        jnp.asarray(unroll_scatter(row_count, col_count), bf16),
         jnp.asarray(small),
         own,
     )
+    scatter = jnp.asarray(unroll_scatter(row_count, col_count), bf16)
     keep, send, own_b, row_b, col_b, diag_b = pl.pallas_call(
         functools.partial(attention_kernel, geo),
         out_shape=[
@@ -743,7 +771,7 @@
             shape((rows_half, 128), f32),
         ]
         + [shape((size, width), bf16) for size in sizes],
-        in_specs=[vmem] * 15,
+        in_specs=[vmem] * 5 + [hbm] + [vmem] * 5 + [hbm, vmem, hbm, vmem],
         out_specs=[vmem] * 6,
         scratch_shapes=[
             pltpu.VMEM((tile_sizes(row_count, col_count)[2], width), bf16),
@@ -758,6 +786,10 @@
             pltpu.VMEM((GROUP + 1, WIN * WIN, 128), f32),
             pltpu.VMEM((GROUP + 1, WIN * WIN, 128), bf16),
             pltpu.VMEM((GROUP + 1, WIN * WIN, 128), bf16),
+            pltpu.VMEM(proj_weight.shape, bf16),
+            pltpu.VMEM(join_block.shape, bf16),
+            pltpu.VMEM(scatter.shape, bf16),
+            pltpu.SemaphoreType.DMA((3,)),
         ],
         compiler_params=pltpu.CompilerParams(vmem_limit_bytes=24 << 20),
         name="window_attention",
@@ -767,27 +799,25 @@
         rc,
         rd,
         near_gather,
-        near_scatter,
+        pltpu.with_memory_space_constraint(scatter, pltpu.HBM),
         ln_gain,
         ln_bias,
-        qkv_weight,
+        near_qkv,
         qkv_bias,
         pair_bias,
-        near_proj,
+        pltpu.with_memory_space_constraint(proj_weight, pltpu.HBM),
         proj_bias,
-        near_join,
+        pltpu.with_memory_space_constraint(join_block, pltpu.HBM),
         near_small,
     )
 
-    rr_b = shifted(row_b, 1, 0)
-    rd_b = shifted(diag_b, 1, 1)
+    rr_b = shifted(row_b, -1, 0)
+    rd_b = shifted(diag_b, -1, 1)
     rc_b = shifted(col_b, 0, 1)
-    mine = keep + exchanged(send, 1)
-    mask = 2
-    while mask < everyone:
-        mine = mine + exchanged(mine, mask)
-        mask *= 2
-    other = exchanged(mine, 1)
+    mine = keep + exchanged(send, (1, 1))
+    for masks in round_masks(everyone):
+        mine = mine + exchanged(mine, masks)
+    other = exchanged(mine, (1, 1))
 
     direct, share = pl.pallas_call(
         functools.partial(direct_kernel, geo),
@@ -840,6 +870,15 @@
     return joined.reshape(row_count, col_count, channels)
 
 
+def round_masks(count):
+    masks = [1 << k for k in range(1, count.bit_length() - 1)]
+    half = len(masks) // 2
+    rounds = []
+    for first, second in zip(masks[:half], masks[half : 2 * half]):
+        rounds += [(first, second), (second, first)]
+    return rounds + [(mask, mask) for mask in masks[2 * half :]]
+
+
 def solution(mesh):
     in_specs = (P("rows", "cols", None),) + (P(),) * 13
     return jax.shard_map(

time: 54.9 us -> 52 us (0.947)
  the two profiles are of different devices: /device:TPU:0 before, /device:TPU:25 now
where the time goes in v2:
time: 52 us; the launch traced here: 51.8 us
  waiting for transfers between devices  24.2 us (47%)
  Pallas kernels  14 us (27%)
  starting transfers between devices  13.2 us (25%)
    ppermute x6, waiting for transfers between devices, exchanged(): lax.ppermute(value, axes, [(i, i ^ masks[i % 2]) for i in range(everyone)])  15.9 us
    ppermute x6, starting transfers between devices, exchanged(): lax.ppermute(value, axes, [(i, i ^ masks[i % 2]) for i in range(everyone)])  9.64 us
    ppermute x6, waiting for transfers between devices, shifted(): return lax.ppermute(value, axes, pairs)  8.29 us
    pallas_call x1, Pallas kernels, shards(): pl.pallas_call(functools.partial(attention_kernel, geo), out_shape=[shape...  6.76 us
    ppermute x6, starting transfers between devices, shifted(): return lax.ppermute(value, axes, pairs)  3.53 us
    pallas_call x1, Pallas kernels, expanded_bias(): pl.pallas_call(functools.partial(bias_kernel, len(brought)), out_shape=[j...  2.59 us
    pallas_call x1, Pallas kernels, shards(): pl.pallas_call(functools.partial(final_kernel, geo), out_shape=shape((cou...  2.48 us
    pallas_call x1, Pallas kernels, shards(): pl.pallas_call(functools.partial(send_kernel, geo), out_shape=[shape((siz...  1.56 us
  transfers between devices with their start and end apart: 12, of which 9 were waited for; matrix products, arithmetic and copies ran while one was open for 0% of the time, Pallas kernels for 6%

profile of v2, /device:TPU:25, one launch (start us, length us, event | category | flops | bytes accessed | tf_op | source)
XLA Modules:
  0.0 51.8 jit_solution(15429600480371618477)
XLA Ops:
  0.0 1.6 %send_pieces.1 = (bf16[108,768]{1,0:T(8,128)(2,1)S(1)}, bf16[36,768]{1,0:T(8,128)(2,1)S(1)}, bf16[36,768]{1,0:T(8,128)(2,1)S(1)}, f32[23,23,24]{2,1,0:T(8,128)S(1)}) custom-call(bf16[288,768]{1,0:T(8,128)(2,1)} %bitcast.2, bf16[208,288]{1,0:T(8,128)(2,1)} %constant.18.clone.table_ref, f32[23,23,24]{2,1,0:T(8,128)} %rel_ref.1), custom_call_target="tpu_custom_call" | custom-call | tf_op jit(solution)/shard_map/send_pieces/pallas_call | solution.py:720
  1.6 1.3 %collective-permute-start = (bf16[108,768]{1,0:T(8,128)(2,1)S(1)}, bf16[108,768]{1,0:T(8,128)(2,1)S(1)}, u32[]{:S(2)}, u32[]{:S(2)}) collective-permute-start(bf16[108,768]{1,0:T(8,128)(2,1)S(1)} %get-tuple-element.24), channel_id=1, source_target_pairs={{0,4},{1,5},{2,6},{3,7},{4,8},{5,9},{6,10},{7,11},{8,12},{9,13},{1... | collective-permute-start | bytes 497672 | tf_op jit(solution)/shard_map/ppermute | solution.py:709
  2.9 1.0 %collective-permute-start.1 = (bf16[36,768]{1,0:T(8,128)(2,1)S(1)}, bf16[36,768]{1,0:T(8,128)(2,1)S(1)}, u32[]{:S(2)}, u32[]{:S(2)}) collective-permute-start(bf16[36,768]{1,0:T(8,128)(2,1)S(1)} %get-tuple-element.25), channel_id=1, source_target_pairs={{0,3},{1,0},{2,1},{3,2},{4,7},{5,4},{6,5},{7,6},{8,11},{9,8},{10,9... | collective-permute-start | bytes 165896 | tf_op jit(solution)/shard_map/ppermute | solution.py:709
  3.8 0.6 %collective-permute-start.2 = (bf16[36,768]{1,0:T(8,128)(2,1)S(1)}, bf16[36,768]{1,0:T(8,128)(2,1)S(1)}, u32[]{:S(2)}, u32[]{:S(2)}) collective-permute-start(bf16[36,768]{1,0:T(8,128)(2,1)S(1)} %get-tuple-element.26), channel_id=1, source_target_pairs={{0,7},{1,4},{2,5},{3,6},{4,11},{5,8},{6,9},{7,10},{8,15},{9,12},{1... | collective-permute-start | bytes 165896 | tf_op jit(solution)/shard_map/ppermute | solution.py:709
  4.4 2.6 %expand_bias.1 = (f32[27,144,128]{2,1,0:T(8,128)S(1)}, bf16[768,2304]{1,0:T(8,128)(2,1)S(1)}, bf16[288,496]{1,0:T(8,128)(2,1)S(1)}, f32[128,384]{1,0:T(8,128)S(1)}, bf16[288,768]{1,0:T(8,128)(2,1)S(1)}) custom-call(f32[23,23,24]{2,1,0:T(8,128)S(1)} %get-tuple-element.22.table_ref, bf16[768,2304]{1,0:T(8,128)(2,1)} %refs_0_.1, ...), custom_call_target="tpu_custom_call" | custom-call | flops 1990656 | bytes 1990656 | tf_op jit(solution)/shard_map/expand_bias/pallas_call | solution.py:333
  7.0 0.1 collective-permute-done.1.rc_ref
  7.1 3.8 %collective-permute-done.2.rd_ref = bf16[36,768]{1,0:T(8,128)(2,1)S(1)} collective-permute-done((bf16[36,768]{1,0:T(8,128)(2,1)S(1)}, bf16[36,768]{1,0:T(8,128)(2,1)S(1)}, u32[]{:S(2)}, u32[]{:S(2)}) %collective-permute-start.2) | collective-permute-done | bytes 55328 | tf_op jit(solution)/shard_map/ppermute | solution.py:709
  10.9 0.0 copy-start
  10.9 0.0 copy-start.3
  10.9 0.0 copy-start.5
  10.9 0.0 copy-start.12
  11.0 0.0 copy-start.2
  11.0 0.0 copy-start.4
  11.0 6.8 %window_attention.1 = (f32[200,128]{1,0:T(8,128)S(1)}, f32[200,128]{1,0:T(8,128)S(1)}, bf16[108,768]{1,0:T(8,128)(2,1)S(1)}, bf16[108,768]{1,0:T(8,128)(2,1)S(1)...) custom-call(bf16[288,768]{1,0:T(8,128)(2,1)S(1)} %get-tuple-element.23.own_ref, ...), custom_call_target="tpu_custom_call" | custom-call | tf_op jit(solution)/shard_map/window_attention/pallas_call | solution.py:767
  17.8 0.0 copy-start.6
  17.8 0.1 collective-permute-start.3
  17.9 1.3 %collective-permute-done.3 = f32[200,128]{1,0:T(8,128)S(1)} collective-permute-done((f32[200,128]{1,0:T(8,128)S(1)}, f32[200,128]{1,0:T(8,128)S(1)}, u32[]{:S(2)}, u32[]{:S(2)}) %collective-permute-start.3) | collective-permute-done | bytes 102432 | tf_op jit(solution)/shard_map/ppermute | solution.py:712
  19.2 0.2 collective-permute-start.4
  19.4 3.6 %collective-permute-done.4 = f32[200,128]{1,0:T(8,128)S(1)} collective-permute-done((f32[200,128]{1,0:T(8,128)S(1)}, f32[200,128]{1,0:T(8,128)S(1)}, u32[]{:S(2)}, u32[]{:S(2)}) %collective-permute-start.4) | collective-permute-done | bytes 102432 | tf_op jit(solution)/shard_map/ppermute | solution.py:712
  23.1 0.3 collective-permute-start.5
  23.4 3.2 %collective-permute-done.5 = f32[200,128]{1,0:T(8,128)S(1)} collective-permute-done((f32[200,128]{1,0:T(8,128)S(1)}, f32[200,128]{1,0:T(8,128)S(1)}, u32[]{:S(2)}, u32[]{:S(2)}) %collective-permute-start.5) | collective-permute-done | bytes 102432 | tf_op jit(solution)/shard_map/ppermute | solution.py:712
  26.7 0.7 %collective-permute-start.6 = (f32[200,128]{1,0:T(8,128)S(1)}, f32[200,128]{1,0:T(8,128)S(1)}, u32[]{:S(2)}, u32[]{:S(2)}) collective-permute-start(f32[200,128]{1,0:T(8,128)S(1)} %add.17), channel_id=1, source_target_pairs={{0,4},{1,17},{2,6},{3,19},{4,0},{5,21},{6,2},{7,23},{8,12},{9,25},... | collective-permute-start | bytes 307208 | tf_op jit(solution)/shard_map/ppermute | solution.py:712
  27.4 4.7 %collective-permute-done.6 = f32[200,128]{1,0:T(8,128)S(1)} collective-permute-done((f32[200,128]{1,0:T(8,128)S(1)}, f32[200,128]{1,0:T(8,128)S(1)}, u32[]{:S(2)}, u32[]{:S(2)}) %collective-permute-start.6) | collective-permute-done | bytes 102432 | tf_op jit(solution)/shard_map/ppermute | solution.py:712
  32.2 0.1 collective-permute-start.7
  32.2 0.5 collective-permute-start.9
  32.7 3.0 %collective-permute-done.7 = f32[200,128]{1,0:T(8,128)S(1)} collective-permute-done((f32[200,128]{1,0:T(8,128)S(1)}, f32[200,128]{1,0:T(8,128)S(1)}, u32[]{:S(2)}, u32[]{:S(2)}) %collective-permute-start.7) | collective-permute-done | bytes 102432 | tf_op jit(solution)/shard_map/ppermute | solution.py:712
  35.8 8.2 %collective-permute-start.8 = (f32[200,128]{1,0:T(8,128)S(1)}, f32[200,128]{1,0:T(8,128)S(1)}, u32[]{:S(2)}, u32[]{:S(2)}) collective-permute-start(f32[200,128]{1,0:T(8,128)S(1)} %add.19.mine_ref), channel_id=1, source_target_pairs={{0,1},{1,0},{2,3},{3,2},{4,5},{5,4},{6,7},{7,6},{8,9},{9,8},{10,11... | collective-permute-start | bytes 307208 | tf_op jit(solution)/shard_map/ppermute | solution.py:712
  44.0 0.2 collective-permute-start.10
  44.2 1.8 %collective-permute-done.10.rc_ref = bf16[36,768]{1,0:T(8,128)(2,1)S(1)} collective-permute-done((bf16[36,768]{1,0:T(8,128)(2,1)S(1)}, bf16[36,768]{1,0:T(8,128)(2,1)S(1)}, u32[]{:S(2)}, u32[]{:S(2)}) %collective-permute-start.10) | collective-permute-done | bytes 55328 | tf_op jit(solution)/shard_map/ppermute | solution.py:709
  46.0 2.6 %collective-permute-done.11.rd_ref = bf16[36,768]{1,0:T(8,128)(2,1)S(1)} collective-permute-done((bf16[36,768]{1,0:T(8,128)(2,1)S(1)}, bf16[36,768]{1,0:T(8,128)(2,1)S(1)}, u32[]{:S(2)}, u32[]{:S(2)}) %collective-permute-start.11) | collective-permute-done | bytes 55328 | tf_op jit(solution)/shard_map/ppermute | solution.py:709
  48.7 0.6 %direct_join.1 = (f32[288,512]{1,0:T(8,128)S(1)}, bf16[288,256]{1,0:T(8,128)(2,1)S(1)}) custom-call(bf16[108,768]{1,0:T(8,128)(2,1)S(1)} %get-tuple-element.33.own_ref, bf16[108,768]{1,0:T(8,128)(2,1)S(1)} %collective-permute-done.9.rr_ref, bf16[36,768]{1,0:T(8,128)(2,1)S(1)} %collective-permute-done.10.rc_ref, ...), custom_call_target="tpu_custom_call" | custom-call | flops 226492416 | bytes 4194304 | tf_op jit(solution)/shard_map/direct_join/pallas_call | solution.py:822
  49.4 2.5 %final_join.1 = bf16[288,512]{1,0:T(8,128)(2,1)} custom-call(f32[200,128]{1,0:T(8,128)S(1)} %add.19.mine_ref, f32[200,128]{1,0:T(8,128)S(1)} %collective-permute-done.8.other_ref, f32[288,512]{1,0:T(8,128)S(1)} %get-tuple-element.37.direct_ref, bf16[288,256]{1,0:T(8,128)(2,1)S(1)} %get-tuple-element.38.share_ref, bf16[4,768,512]{2,1,0:T(8,128)(2,1)S(1)} %copy-done.1, ...), custom_call_target="tpu_custom_call" | custom-call | tf_op jit(solution)/shard_map/final_join/pallas_call | solution.py:844
  (32 shorter events, 0.1 us)
Async XLA Ops:
  0.0 10.9 %copy-start.11 = (f32[768]{0:T(1024)S(1)}, f32[768]{0:T(1024)}, u32[]{:S(2)}) copy-start(f32[768]{0:T(1024)} %bproj_ref.1) | copy-start | bytes 9220
  0.0 10.9 %copy-start.7 = (f32[2304]{0:T(1024)S(1)}, f32[2304]{0:T(1024)}, u32[]{:S(2)}) copy-start(f32[2304]{0:T(1024)} %bqkv_ref.1) | copy-start | bytes 27652
  0.0 10.9 %copy-start.10 = (f32[768]{0:T(1024)S(1)}, f32[768]{0:T(1024)}, u32[]{:S(2)}) copy-start(f32[768]{0:T(1024)} %lnb_ref.1) | copy-start | bytes 9220
  0.0 10.9 %copy-start.9 = (f32[768]{0:T(1024)S(1)}, f32[768]{0:T(1024)}, u32[]{:S(2)}) copy-start(f32[768]{0:T(1024)} %lng_ref.1) | copy-start | bytes 9220
  1.6 9.3 %collective-permute-start = (bf16[108,768]{1,0:T(8,128)(2,1)S(1)}, bf16[108,768]{1,0:T(8,128)(2,1)S(1)}, u32[]{:S(2)}, u32[]{:S(2)}) collective-permute-start(bf16[108,768]{1,0:T(8,128)(2,1)S(1)} %get-tuple-element.24), channel_id=1, source_target_pairs={{0,4},{1,5},{2,6},{3,7},{4,8},{5,9},{6,10},{7,11},{8,12},{9,13},{1... | collective-permute-start | bytes 497672 | tf_op jit(solution)/shard_map/ppermute | solution.py:709
  2.9 4.2 %collective-permute-start.1 = (bf16[36,768]{1,0:T(8,128)(2,1)S(1)}, bf16[36,768]{1,0:T(8,128)(2,1)S(1)}, u32[]{:S(2)}, u32[]{:S(2)}) collective-permute-start(bf16[36,768]{1,0:T(8,128)(2,1)S(1)} %get-tuple-element.25), channel_id=1, source_target_pairs={{0,3},{1,0},{2,1},{3,2},{4,7},{5,4},{6,5},{7,6},{8,11},{9,8},{10,9... | collective-permute-start | bytes 165896 | tf_op jit(solution)/shard_map/ppermute | solution.py:709
  3.8 7.0 %collective-permute-start.2 = (bf16[36,768]{1,0:T(8,128)(2,1)S(1)}, bf16[36,768]{1,0:T(8,128)(2,1)S(1)}, u32[]{:S(2)}, u32[]{:S(2)}) collective-permute-start(bf16[36,768]{1,0:T(8,128)(2,1)S(1)} %get-tuple-element.26), channel_id=1, source_target_pairs={{0,7},{1,4},{2,5},{3,6},{4,11},{5,8},{6,9},{7,10},{8,15},{9,12},{1... | collective-permute-start | bytes 165896 | tf_op jit(solution)/shard_map/ppermute | solution.py:709
  10.9 37.7 %copy-start = (bf16[768,512]{1,0:T(8,128)(2,1)S(1)}, bf16[768,512]{1,0:T(8,128)(2,1)}, u32[]{:S(2)}) copy-start(bf16[768,512]{1,0:T(8,128)(2,1)} %wjoin_ref.1) | copy-start | bytes 2359300
  10.9 37.7 %copy-start.3 = (bf16[288,320]{1,0:T(8,128)(2,1)S(1)}, bf16[288,320]{1,0:T(8,128)(2,1)}, u32[]{:S(2)}) copy-start(bf16[288,320]{1,0:T(8,128)(2,1)} %constant.22.clone.gather_ref) | copy-start | bytes 552964
  10.9 37.7 %copy-start.5 = (f32[288,8]{1,0:T(8,128)S(1)}, f32[288,8]{1,0:T(8,128)}, u32[]{:S(2)}) copy-start(f32[288,8]{1,0:T(8,128)} %constant.23.clone.token_ref) | copy-start | bytes 27652
  10.9 37.7 %copy-start.12 = (f32[8,128]{1,0:T(8,128)S(1)}, f32[8,128]{1,0:T(8,128)}, u32[]{:S(2)}) copy-start(f32[8,128]{1,0:T(8,128)} %constant.24.clone.cell_ref) | copy-start | bytes 12292
  11.0 38.3 %copy-start.2 = (bf16[4,512,512]{2,1,0:T(8,128)(2,1)S(1)}, bf16[4,512,512]{2,1,0:T(8,128)(2,1)}, u32[]{:S(2)}) copy-start(bf16[4,512,512]{2,1,0:T(8,128)(2,1)} %jb_ref.1) | copy-start | bytes 6291460
  11.0 38.3 %copy-start.4 = (bf16[336,192]{1,0:T(8,128)(2,1)S(1)}, bf16[336,192]{1,0:T(8,128)(2,1)}, u32[]{:S(2)}) copy-start(bf16[336,192]{1,0:T(8,128)(2,1)} %constant.26.clone.gram_ref) | copy-start | bytes 387076
  17.8 31.6 %copy-start.1 = (bf16[4,768,512]{2,1,0:T(8,128)(2,1)S(1)}, bf16[4,768,512]{2,1,0:T(8,128)(2,1)}, u32[]{:S(2)}) copy-start(bf16[4,768,512]{2,1,0:T(8,128)(2,1)} %wb_ref.1) | copy-start | bytes 9437188
  17.8 31.6 %copy-start.6 = (bf16[72,120]{1,0:T(8,128)(2,1)S(1)}, bf16[72,120]{1,0:T(8,128)(2,1)}, u32[]{:S(2)}) copy-start(bf16[72,120]{1,0:T(8,128)(2,1)} %constant.25.clone.group_ref) | copy-start | bytes 51844
  17.8 31.6 %copy-start.8 = (f32[4,512]{1,0:T(4,128)S(1)}, f32[4,512]{1,0:T(4,128)}, u32[]{:S(2)}) copy-start(f32[4,512]{1,0:T(4,128)} %bb_ref.1) | copy-start | bytes 24580
  17.8 31.5 %copy-start.13 = (f32[512]{0:T(512)S(1)}, f32[512]{0:T(512)}, u32[]{:S(2)}) copy-start(f32[512]{0:T(512)} %gain_ref.1) | copy-start | bytes 6148
  17.8 31.5 %copy-start.14 = (f32[512]{0:T(512)S(1)}, f32[512]{0:T(512)}, u32[]{:S(2)}) copy-start(f32[512]{0:T(512)} %bias_ref.1) | copy-start | bytes 6148
  17.8 1.4 %collective-permute-start.3 = (f32[200,128]{1,0:T(8,128)S(1)}, f32[200,128]{1,0:T(8,128)S(1)}, u32[]{:S(2)}, u32[]{:S(2)}) collective-permute-start(f32[200,128]{1,0:T(8,128)S(1)} %get-tuple-element.32), channel_id=1, source_target_pairs={{0,1},{1,0},{2,3},{3,2},{4,5},{5,4},{6,7},{7,6},{8,9},{9,8},{10,11... | collective-permute-start | bytes 307208 | tf_op jit(solution)/shard_map/ppermute | solution.py:712
  19.2 3.9 %collective-permute-start.4 = (f32[200,128]{1,0:T(8,128)S(1)}, f32[200,128]{1,0:T(8,128)S(1)}, u32[]{:S(2)}, u32[]{:S(2)}) collective-permute-start(f32[200,128]{1,0:T(8,128)S(1)} %add.15), channel_id=1, source_target_pairs={{0,2},{1,9},{2,0},{3,11},{4,6},{5,13},{6,4},{7,15},{8,10},{9,1},{1... | collective-permute-start | bytes 307208 | tf_op jit(solution)/shard_map/ppermute | solution.py:712
  23.1 3.6 %collective-permute-start.5 = (f32[200,128]{1,0:T(8,128)S(1)}, f32[200,128]{1,0:T(8,128)S(1)}, u32[]{:S(2)}, u32[]{:S(2)}) collective-permute-start(f32[200,128]{1,0:T(8,128)S(1)} %add.16), channel_id=1, source_target_pairs={{0,8},{1,3},{2,10},{3,1},{4,12},{5,7},{6,14},{7,5},{8,0},{9,11},{1... | collective-permute-start | bytes 307208 | tf_op jit(solution)/shard_map/ppermute | solution.py:712
  26.7 5.5 %collective-permute-start.6 = (f32[200,128]{1,0:T(8,128)S(1)}, f32[200,128]{1,0:T(8,128)S(1)}, u32[]{:S(2)}, u32[]{:S(2)}) collective-permute-start(f32[200,128]{1,0:T(8,128)S(1)} %add.17), channel_id=1, source_target_pairs={{0,4},{1,17},{2,6},{3,19},{4,0},{5,21},{6,2},{7,23},{8,12},{9,25},... | collective-permute-start | bytes 307208 | tf_op jit(solution)/shard_map/ppermute | solution.py:712
  32.2 3.6 %collective-permute-start.7 = (f32[200,128]{1,0:T(8,128)S(1)}, f32[200,128]{1,0:T(8,128)S(1)}, u32[]{:S(2)}, u32[]{:S(2)}) collective-permute-start(f32[200,128]{1,0:T(8,128)S(1)} %add.18), channel_id=1, source_target_pairs={{0,16},{1,5},{2,18},{3,7},{4,20},{5,1},{6,22},{7,3},{8,24},{9,13},... | collective-permute-start | bytes 307208 | tf_op jit(solution)/shard_map/ppermute | solution.py:712
  32.2 16.4 %collective-permute-start.9 = (bf16[108,768]{1,0:T(8,128)(2,1)S(1)}, bf16[108,768]{1,0:T(8,128)(2,1)S(1)}, u32[]{:S(2)}, u32[]{:S(2)}) collective-permute-start(bf16[108,768]{1,0:T(8,128)(2,1)S(1)} %get-tuple-element.34), channel_id=1, source_target_pairs={{0,28},{1,29},{2,30},{3,31},{4,0},{5,1},{6,2},{7,3},{8,4},{9,5},{1... | collective-permute-start | bytes 497672 | tf_op jit(solution)/shard_map/ppermute | solution.py:709
  35.8 13.5 %collective-permute-start.8 = (f32[200,128]{1,0:T(8,128)S(1)}, f32[200,128]{1,0:T(8,128)S(1)}, u32[]{:S(2)}, u32[]{:S(2)}) collective-permute-start(f32[200,128]{1,0:T(8,128)S(1)} %add.19.mine_ref), channel_id=1, source_target_pairs={{0,1},{1,0},{2,3},{3,2},{4,5},{5,4},{6,7},{7,6},{8,9},{9,8},{10,11... | collective-permute-start | bytes 307208 | tf_op jit(solution)/shard_map/ppermute | solution.py:712
  44.0 2.1 %collective-permute-start.10 = (bf16[36,768]{1,0:T(8,128)(2,1)S(1)}, bf16[36,768]{1,0:T(8,128)(2,1)S(1)}, u32[]{:S(2)}, u32[]{:S(2)}) collective-permute-start(bf16[36,768]{1,0:T(8,128)(2,1)S(1)} %get-tuple-element.35), channel_id=1, source_target_pairs={{0,1},{1,2},{2,3},{3,0},{4,5},{5,6},{6,7},{7,4},{8,9},{9,10},{10,1... | collective-permute-start | bytes 165896 | tf_op jit(solution)/shard_map/ppermute | solution.py:709
  44.2 4.4 %collective-permute-start.11 = (bf16[36,768]{1,0:T(8,128)(2,1)S(1)}, bf16[36,768]{1,0:T(8,128)(2,1)S(1)}, u32[]{:S(2)}, u32[]{:S(2)}) collective-permute-start(bf16[36,768]{1,0:T(8,128)(2,1)S(1)} %get-tuple-element.36), channel_id=1, source_target_pairs={{0,29},{1,30},{2,31},{3,28},{4,1},{5,2},{6,3},{7,0},{8,5},{9,6},{1... | collective-permute-start | bytes 165896 | tf_op jit(solution)/shard_map/ppermute | solution.py:709
